TPU v7x, 32 devices: a whole 2x2x4 slice. The times are simulated.
32 devices in a mesh: clip: 8 (over z, x), cap: 4 (over y, core).
Axes of the slice: x: 2, y: 2, z: 4, core: 2. Of those that a mesh axis runs over, the one named last changes fastest.
Arguments:
- text: bfloat16 [128, 512], replicated, may hold values from -8 to 8
- patches: bfloat16 [16, 16, 196, 512], P('clip', None, 'cap'), may hold values from -6 to 6
- frame_slots: int32 [16, 16], P('clip'), may hold values from -1 to 127, as said below
Outputs:
- contrast_loss: float32 [], replicated
- patch_grad: bfloat16 [16, 16, 196, 512], P('clip', None, 'cap')
- text_grad: float32 [128, 512], P(('clip', 'cap'))
Inputs may be any that keep to these rules, and one draw needn't show every extreme that they name: `frame_slots`: in every clip the valid frames are the first 4 to 16 slots, and on some index of clip every clip has all 16; all clips together have 16 * 8 valid frames. A valid entry is t * 16 + s: the frame goes to index t of clip, slot s; every index of clip receives exactly 16 frames, one in each slot. A frame stays on its own index of clip unless that index holds more than 16 frames; then its frames past the first 16, in clip and frame order, go to other indices. At most 3 frames go from one index of clip to another, a bound that some pair reaches.
All inputs are finite; a program needn't handle non-finite values.
Results may differ from a plain program's by a relative error of at most 0.0065.
Values may be sent and summed in bfloat16 or wider, within the bound.
No kernel may reach another device: no remote copies, remote signals or barrier semaphores. Data moves between devices by JAX's collectives and lax.ppermute only.
A program may use at most 64 MiB of HBM per device.

v0:
```python
import jax
import jax.numpy as jnp
from jax import lax
from jax.sharding import PartitionSpec as P

WORDS = 8


logit_scale = 32.0
loss_scale = 8192.0
big_value = 1e30


def block_stats(scores, usable):
    maximum = jnp.max(jnp.where(usable, scores, -big_value), axis=2)
    weight = jnp.where(usable, jnp.exp(scores - maximum[..., None]), 0.0)
    return (maximum, jnp.sum(weight, axis=2), jnp.sum(weight * scores, axis=2))


def merge_groups(maxima, totals, numerators, member):
    inside = member[:, :, None]
    merged_max = jnp.max(jnp.where(inside, maxima[None], -big_value), axis=1)
    factor = jnp.where(inside, jnp.exp(maxima[None] - merged_max[:, None]), 0.0)
    merged_sum = jnp.sum(factor * totals[None], axis=1)
    merged_num = jnp.sum(factor * numerators[None], axis=1)
    return (merged_max, merged_sum, merged_num)


def per_device(text, patches, frame_slots):
    clip_devices = lax.axis_size("clip")
    cap_devices = lax.axis_size("cap")
    my_rank = lax.axis_index("clip")
    local_clips, frame_max, patch_rows, width = patches.shape
    text_rows = text.shape[0]
    clip_total = clip_devices * local_clips
    quarter = text_rows // cap_devices
    factor_scale = width ** (-0.5)
    frame_total = local_clips * frame_max
    flat_frames = patches.reshape(frame_total, patch_rows, width)
    own_flat = flat_frames.reshape(-1, width)
    scores = (
        lax.dot_general(
            text, own_flat, (((1,), (1,)), ((), ())), preferred_element_type=jnp.float32
        )
        * factor_scale
    )
    scores = scores.reshape(text_rows, local_clips, frame_max * patch_rows)
    usable = jnp.repeat(frame_slots >= 0, patch_rows, axis=1)[None]
    maximum, totals, weighted = block_stats(scores, usable)
    got_max, got_sum, got_num = (
        lax.all_to_all(maximum.T, "cap", split_axis=1, concat_axis=0, tiled=True),
        lax.all_to_all(totals.T, "cap", split_axis=1, concat_axis=0, tiled=True),
        lax.all_to_all(weighted.T, "cap", split_axis=1, concat_axis=0, tiled=True),
    )
    member = jnp.tile(jnp.eye(local_clips, dtype=bool), (1, cap_devices))
    merged_max, merged_sum, merged_num = merge_groups(got_max, got_sum, got_num, member)
    pooled = merged_num / merged_sum
    gathered_max, gathered_sum, gathered_pool = (
        lax.all_gather(merged_max[None], ("clip", "cap"), axis=0, tiled=True),
        lax.all_gather(merged_sum[None], ("clip", "cap"), axis=0, tiled=True),
        lax.all_gather(pooled[None], ("clip", "cap"), axis=0, tiled=True),
    )

    def arrange(stacked):
        return (
            stacked.reshape(clip_devices, cap_devices, local_clips, quarter)
            .transpose(0, 2, 1, 3)
            .reshape(clip_total, text_rows)
        )

    all_max = arrange(gathered_max)
    all_sum = arrange(gathered_sum)
    all_pool = arrange(gathered_pool)
    similar = jnp.mean(all_pool.reshape(clip_total, clip_total, WORDS), axis=2)
    logits = logit_scale * similar.T
    row_terms = jax.nn.logsumexp(logits, axis=1)
    col_terms = jax.nn.logsumexp(logits, axis=0)
    matched = jnp.diagonal(logits)
    contrast_loss = 0.5 * (jnp.mean(row_terms - matched) + jnp.mean(col_terms - matched))
    identity = jnp.eye(clip_total, dtype=logits.dtype)
    grad_logits = (
        loss_scale
        * 0.5
        / clip_total
        * (jax.nn.softmax(logits, axis=1) + jax.nn.softmax(logits, axis=0) - 2.0 * identity)
    )
    grad_pooled = jnp.repeat(logit_scale / WORDS * grad_logits.T, WORDS, axis=1)
    first_clip = my_rank * local_clips
    max_rows = lax.dynamic_slice_in_dim(all_max, first_clip, local_clips, 0).T[:, :, None]
    sum_rows = lax.dynamic_slice_in_dim(all_sum, first_clip, local_clips, 0).T[:, :, None]
    pool_rows = lax.dynamic_slice_in_dim(all_pool, first_clip, local_clips, 0).T[:, :, None]
    grad_rows = lax.dynamic_slice_in_dim(grad_pooled, first_clip, local_clips, 0).T[:, :, None]
    weights = jnp.where(usable, jnp.exp(scores - max_rows) / sum_rows, 0.0)
    grad_scores = (grad_rows * weights * (1.0 + scores - pool_rows)).astype(jnp.bfloat16)
    grad_flat = grad_scores.reshape(text_rows, frame_total * patch_rows)
    frame_grad = (
        lax.dot_general(
            grad_flat, text, (((0,), (0,)), ((), ())), preferred_element_type=jnp.float32
        )
        * factor_scale
    )
    frame_grad = frame_grad.astype(jnp.bfloat16).reshape(patches.shape)
    text_part = (
        lax.dot_general(
            grad_flat, own_flat, (((1,), (0,)), ((), ())), preferred_element_type=jnp.float32
        )
        * factor_scale
    )
    text_grad = lax.psum_scatter(text_part, ("clip", "cap"), scatter_dimension=0, tiled=True)
    return (contrast_loss, frame_grad, text_grad)


def solution(mesh):
    return jax.shard_map(
        per_device,
        mesh=mesh,
        in_specs=(P(), P("clip", None, "cap", None), P("clip", None)),
        out_specs=(P(), P("clip", None, "cap", None), P(("clip", "cap"), None)),
        check_vma=False,
    )
```

profile of v0, /device:TPU:0, one launch (start us, length us, event | category | flops | bytes accessed | tf_op | source)
XLA Modules:
  0.0 287.9 jit_solution(9972560687561934756)
XLA Ops:
  7.2 0.0 copy-start
  7.2 0.7 broadcast_compare_fusion
  7.9 0.1 broadcast_in_dim.92
  8.0 0.1 broadcast_in_dim.93
  8.1 3.6 %copy.34 = bf16[2,16,49,512]{3,2,1,0:T(8,128)(2,1)} copy(bf16[2,16,49,512]{3,1,2,0:T(8,128)(2,1)} %param.4) | data formatting | bytes 3211264 | tf_op args[1]
  11.6 1.7 reshape_reshape.6
  13.4 0.0 copy-done
  13.4 0.6 convolution_multiply_fusion.1
  14.0 0.3 select_reduce_fusion
  14.3 0.3 fusion.6
  14.6 0.1 all_to_all.42
  14.6 0.6 copy.37
  15.2 4.3 %all-to-all-start.2 = ((f32[2,4,32]{2,0,1:T(2,128)}), f32[2,4,32]{2,0,1:T(2,128)S(1)}, u32[]{:S(2)}, u32[]{:S(2)}) async-start(f32[2,4,32]{2,0,1:T(2,128)} %copy.37), calls=%async_computation.2 | async-start | bytes 8192 | tf_op jit(solution)/shard_map/all_to_all | solution.py:52
  19.5 0.1 broadcast_in_dim.100
  19.7 0.1 all_to_all.36
  19.8 0.6 copy.35
  20.4 3.0 %all-to-all-done.2 = f32[2,4,32]{2,0,1:T(2,128)S(1)} async-done(((f32[2,4,32]{2,0,1:T(2,128)}), f32[2,4,32]{2,0,1:T(2,128)S(1)}, u32[]{:S(2)}, u32[]{:S(2)}) %all-to-all-start.2) | async-done | bytes 1056 | tf_op jit(solution)/shard_map/all_to_all | solution.py:52
  23.3 3.2 %all-to-all-start = ((f32[2,4,32]{2,0,1:T(2,128)}), f32[2,4,32]{2,0,1:T(2,128)S(1)}, u32[]{:S(2)}, u32[]{:S(2)}) async-start(f32[2,4,32]{2,0,1:T(2,128)} %copy.35), calls=%async_computation | async-start | bytes 8192 | tf_op jit(solution)/shard_map/all_to_all | solution.py:51
  26.6 0.1 tile.13
  26.7 0.1 all_to_all.39
  26.7 0.6 copy.36
  27.3 3.0 %all-to-all-done = f32[2,4,32]{2,0,1:T(2,128)S(1)} async-done(((f32[2,4,32]{2,0,1:T(2,128)}), f32[2,4,32]{2,0,1:T(2,128)S(1)}, u32[]{:S(2)}, u32[]{:S(2)}) %all-to-all-start) | async-done | bytes 1056 | tf_op jit(solution)/shard_map/all_to_all | solution.py:51
  30.3 3.2 %all-to-all-start.1 = ((f32[2,4,32]{2,0,1:T(2,128)}), f32[2,4,32]{2,0,1:T(2,128)S(1)}, u32[]{:S(2)}, u32[]{:S(2)}) async-start(f32[2,4,32]{2,0,1:T(2,128)} %copy.36), calls=%async_computation.1 | async-start | bytes 8192 | tf_op jit(solution)/shard_map/all_to_all | solution.py:53
  33.6 0.0 all-reduce.3.cloned.1.call-start
  33.6 0.1 select_reduce_fusion.1
  33.7 3.6 %all-to-all-done.1 = f32[2,4,32]{2,0,1:T(2,128)S(1)} async-done(((f32[2,4,32]{2,0,1:T(2,128)}), f32[2,4,32]{2,0,1:T(2,128)S(1)}, u32[]{:S(2)}, u32[]{:S(2)}) %all-to-all-start.1) | async-done | bytes 1056 | tf_op jit(solution)/shard_map/all_to_all | solution.py:53
  37.3 0.1 multiply_reduce_fusion.1
  37.4 40.8 %all-gather.3 = f32[32,2,32]{2,1,0:T(2,128)S(1)} all-gather(f32[1,2,32]{2,1,0:T(2,128)S(1)} %divide_bitcast_fusion), channel_id=4, replica_groups=mesh['clip'=8,'cap'=4] {'clip','cap'}, dimensions={0}, use_global_device_ids=true | all-gather | bytes 8448 | tf_op jit(solution)/shard_map/all_gather | solution.py:61
  78.2 0.1 reshape.104
  78.3 0.1 reshape_reshape.7
  78.4 36.7 %all-gather.4 = f32[32,2,32]{2,1,0:T(2,128)S(1)} all-gather(f32[1,2,32]{2,1,0:T(2,128)S(1)} %bitcast.94), channel_id=2, replica_groups=mesh['clip'=8,'cap'=4] {'clip','cap'}, dimensions={0}, use_global_device_ids=true | all-gather | bytes 8448 | tf_op jit(solution)/shard_map/all_gather | solution.py:59
  115.2 0.1 reshape.101
  115.2 38.0 %all-gather.5 = f32[32,2,32]{2,1,0:T(2,128)S(1)} all-gather(f32[1,2,32]{2,1,0:T(2,128)S(1)} %bitcast.93), channel_id=3, replica_groups=mesh['clip'=8,'cap'=4] {'clip','cap'}, dimensions={0}, use_global_device_ids=true | all-gather | bytes 8448 | tf_op jit(solution)/shard_map/all_gather | solution.py:60
  153.3 0.1 reshape.103
  153.4 0.1 reduce_sum.109
  153.5 0.1 multiply_reduce_fusion.3
  153.6 0.2 exponential_reduce_fusion.1
  153.8 0.1 subtract_multiply_fusion
  153.9 0.1 copy.39
  154.0 0.1 dynamic-slice_bitcast_fusion
  154.1 0.1 copy.40
  154.2 0.3 fusion.2
  154.5 1.2 convolution_multiply_fusion.2
  155.7 0.0 all-reduce.3.cloned.1.call-update
  155.7 1.7 fusion
  157.4 1.7 reshape.105
  159.1 1.7 copy.43
  160.8 0.7 gather_fusion
  161.4 0.6 subtract_reduce_fusion
  163.4 115.2 %all-reduce.3.cloned.1.call-done = f32[128,512]{1,0:T(8,128)} async-done(((f32[128,512]{1,0:T(8,128)}), f32[128,512]{1,0:T(8,128)}) %all-reduce.3.cloned.1.call-update) | async-done | bytes 262160
  278.6 1.3 constant_dynamic-slice_fusion
  (11 shorter events, 0.1 us)
Async XLA Ops:
  7.2 6.2 %copy-start = (bf16[128,512]{1,0:T(8,128)(2,1)S(1)}, bf16[128,512]{1,0:T(8,128)(2,1)}, u32[]{:S(2)}) copy-start(bf16[128,512]{1,0:T(8,128)(2,1)} %param.3) | copy-start | bytes 393220
  15.2 8.1 %all-to-all-start.2 = ((f32[2,4,32]{2,0,1:T(2,128)}), f32[2,4,32]{2,0,1:T(2,128)S(1)}, u32[]{:S(2)}, u32[]{:S(2)}) async-start(f32[2,4,32]{2,0,1:T(2,128)} %copy.37), calls=%async_computation.2 | async-start | bytes 8192 | tf_op jit(solution)/shard_map/all_to_all | solution.py:52
  23.3 7.0 %all-to-all-start = ((f32[2,4,32]{2,0,1:T(2,128)}), f32[2,4,32]{2,0,1:T(2,128)S(1)}, u32[]{:S(2)}, u32[]{:S(2)}) async-start(f32[2,4,32]{2,0,1:T(2,128)} %copy.35), calls=%async_computation | async-start | bytes 8192 | tf_op jit(solution)/shard_map/all_to_all | solution.py:51
  30.3 7.0 %all-to-all-start.1 = ((f32[2,4,32]{2,0,1:T(2,128)}), f32[2,4,32]{2,0,1:T(2,128)S(1)}, u32[]{:S(2)}, u32[]{:S(2)}) async-start(f32[2,4,32]{2,0,1:T(2,128)} %copy.36), calls=%async_computation.1 | async-start | bytes 8192 | tf_op jit(solution)/shard_map/all_to_all | solution.py:53
  33.6 245.0 %all-reduce.3.cloned.1.call-start = ((), (), s32[]{:S(2)}) async-start(), calls=%async_computation.3 | async-start | bytes 524288
Sparse Core Ops, SparseCore 0:
  155.8 122.7 all-reduce.2
where the time goes:
time: 288 us
  waiting for transfers between devices  125 us (43%)
  blocking collectives  116 us (40%)
  between operations  16.6 us (6%)
  local copies, waits for them, and re-layouts  13.7 us (5%)
  starting transfers between devices  10.8 us (4%)
  matrix products  3.46 us (1%)
  other arithmetic  2.96 us (1%)
    unnamed x2, waiting for transfers between devices  115 us
    all_gather x1, blocking collectives, per_device(): lax.all_gather(pooled[None], ('clip', 'cap'), axis=0, tiled=True)  40.8 us
    all_gather x1, blocking collectives, per_device(): lax.all_gather(merged_sum[None], ('clip', 'cap'), axis=0, tiled=True)  38 us
    all_gather x1, blocking collectives, per_device(): lax.all_gather(merged_max[None], ('clip', 'cap'), axis=0, tiled=True)  36.7 us
    unnamed x5, local copies, waits for them, and re-layouts  6.59 us
  transfers between devices with their start and end apart: 4, of which 4 were waited for; matrix products, arithmetic and copies ran while one was open for 3% of the time, Pallas kernels for 0%

commit v1 on v0

v1 whole, which is shorter than its diff:
```python
import jax
import jax.numpy as jnp
from jax import lax
from jax.sharding import PartitionSpec as P

WORDS = 8
AXES = ("clip", "cap")

logit_scale = 32.0
loss_scale = 8192.0
big_value = 1e30


def per_device(text, patches, frame_slots):
    clip_devices = lax.axis_size("clip")
    cap_devices = lax.axis_size("cap")
    devices = clip_devices * cap_devices
    my_rank = lax.axis_index("clip")
    local_clips, frame_max, patch_rows, width = patches.shape
    text_rows = text.shape[0]
    clip_total = clip_devices * local_clips
    captions = text_rows // WORDS
    factor_scale = width ** (-0.5)
    columns = patch_rows * frame_max

    flat = patches.transpose(0, 2, 1, 3).reshape(local_clips * columns, width)
    usable = jnp.broadcast_to((frame_slots >= 0)[:, None, :], (local_clips, patch_rows, frame_max))
    usable = usable.reshape(local_clips, columns, 1)

    scores = lax.dot_general(
        flat, text, (((1,), (1,)), ((), ())), preferred_element_type=jnp.float32
    ) * factor_scale
    scores = scores.reshape(local_clips, columns, text_rows)
    maximum = jnp.max(jnp.where(usable, scores, -big_value), axis=1)
    weight = jnp.where(usable, jnp.exp(scores - maximum[:, None, :]), 0.0)
    total = jnp.sum(weight, axis=1)
    numerator = jnp.sum(weight * scores, axis=1)

    partial = jnp.concatenate([maximum, total, numerator], axis=0)
    sent = jnp.broadcast_to(partial[None], (devices,) + partial.shape)
    got = lax.all_to_all(sent, AXES, split_axis=0, concat_axis=0, tiled=True)
    got = got.reshape(clip_devices, cap_devices, 3, local_clips, text_rows)
    maxima, totals, numerators = got[:, :, 0], got[:, :, 1], got[:, :, 2]
    merged_max = jnp.max(maxima, axis=1)
    factor = jnp.exp(maxima - merged_max[:, None])
    merged_sum = jnp.sum(factor * totals, axis=1)
    merged_num = jnp.sum(factor * numerators, axis=1)
    all_max = merged_max.reshape(clip_total, text_rows)
    all_sum = merged_sum.reshape(clip_total, text_rows)
    all_pool = (merged_num / merged_sum).reshape(clip_total, text_rows)

    by_clip = logit_scale * jnp.mean(all_pool.reshape(clip_total, captions, WORDS), axis=2)
    row_max = jnp.max(by_clip, axis=0, keepdims=True)
    row_exp = jnp.exp(by_clip - row_max)
    row_sum = jnp.sum(row_exp, axis=0, keepdims=True)
    col_max = jnp.max(by_clip, axis=1, keepdims=True)
    col_exp = jnp.exp(by_clip - col_max)
    col_sum = jnp.sum(col_exp, axis=1, keepdims=True)
    identity = jnp.eye(clip_total, dtype=jnp.float32)
    grad_logits = (loss_scale * 0.5 / clip_total) * (
        row_exp / row_sum + col_exp / col_sum - 2.0 * identity
    )
    grad_pooled = jnp.repeat(logit_scale / WORDS * grad_logits, WORDS, axis=1)
    matched = jnp.sum(identity * by_clip)
    contrast_loss = 0.5 / clip_total * (
        jnp.sum(row_max + jnp.log(row_sum)) + jnp.sum(col_max + jnp.log(col_sum)) - 2.0 * matched
    )

    first_clip = my_rank * local_clips

    def own(rows):
        return lax.dynamic_slice_in_dim(rows, first_clip, local_clips, 0)[:, None, :]

    weights = jnp.where(usable, jnp.exp(scores - own(all_max)) / own(all_sum), 0.0)
    grad_scores = (own(grad_pooled) * weights * (1.0 + scores - own(all_pool))).astype(jnp.bfloat16)
    grad_flat = grad_scores.reshape(local_clips * columns, text_rows)
    text_part = lax.dot_general(
        grad_flat, flat, (((0,), (0,)), ((), ())), preferred_element_type=jnp.float32
    )
    text_sent = (text_part * factor_scale).reshape(devices, text_rows // devices, width)
    text_got = lax.all_to_all(text_sent, AXES, split_axis=0, concat_axis=0, tiled=True)
    text_grad = jnp.sum(text_got, axis=0)
    frame_grad = lax.dot_general(
        grad_flat, text, (((1,), (0,)), ((), ())), preferred_element_type=jnp.float32
    )
    frame_grad = (frame_grad * factor_scale).astype(jnp.bfloat16)
    frame_grad = frame_grad.reshape(local_clips, patch_rows, frame_max, width).transpose(0, 2, 1, 3)
    return (contrast_loss, frame_grad, text_grad)


def solution(mesh):
    return jax.shard_map(
        per_device,
        mesh=mesh,
        in_specs=(P(), P("clip", None, "cap", None), P("clip", None)),
        out_specs=(P(), P("clip", None, "cap", None), P(AXES, None)),
        check_vma=False,
    )
```

time: 288 us -> 38.8 us (0.13)
  blocking collectives: 116 us -> 0 us
  waiting for transfers between devices: 125 us -> 14.4 us
  between operations: 16.6 us -> 3.89 us
  local copies, waits for them, and re-layouts: 13.7 us -> 2.53 us
    all_gather x3 -> x0, blocking collectives: 116 us -> none  [the longest x1 40.8 us: per_device(): lax.all_gather(pooled[None], ('clip', 'cap'), axis=0, tiled=True)]
    unnamed x2 -> x0, waiting for transfers between devices: 115 us -> none
    unnamed x5 -> x4, local copies, waits for them, and re-layouts: 6.59 us -> 0.52 us
    all_to_all x3 -> x2, waiting for transfers between devices: 9.55 us -> 14.4 us  [the longest x1 8.1 us: per_device(): got = lax.all_to_all(sent, AXES, split_axis=0, concat_axis=0, tiled=True)]
    all_to_all x3 -> x2, starting transfers between devices: 10.8 us -> 9.91 us  [the longest x1 7.33 us: per_device(): got = lax.all_to_all(sent, AXES, split_axis=0, concat_axis=0, tiled=True)]
  transfers between devices with their start and end apart: 4 -> 2, of which waited for: 4 -> 2; matrix products, arithmetic and copies ran while one was open for 3% -> 6% of each run, Pallas kernels for 0% -> 0%
where the time goes in v1:
time: 38.8 us; the launch traced here: 38.5 us
  waiting for transfers between devices  14.4 us (37%)
  starting transfers between devices  9.91 us (26%)
  other arithmetic  4.1 us (11%)
  between operations  3.89 us (10%)
  matrix products  3.63 us (9%)
  local copies, waits for them, and re-layouts  2.53 us (7%)
    all_to_all x1, waiting for transfers between devices, per_device(): got = lax.all_to_all(sent, AXES, split_axis=0, concat_axis=0, tiled=True)  8.1 us
    all_to_all x1, starting transfers between devices, per_device(): got = lax.all_to_all(sent, AXES, split_axis=0, concat_axis=0, tiled=True)  7.33 us
    all_to_all x1, waiting for transfers between devices, per_device(): lax.all_to_all(text_sent, AXES, split_axis=0, concat_axis=0, tiled=True)  6.28 us
    all_to_all x1, starting transfers between devices, per_device(): lax.all_to_all(text_sent, AXES, split_axis=0, concat_axis=0, tiled=True)  2.58 us
    dot_general x1, matrix products, per_device(): lax.dot_general(grad_flat, text, (((1,), (0,)), ((), ())), preferred_elem...  1.72 us
    dot_general x1, matrix products, per_device(): lax.dot_general(flat, text, (((1,), (1,)), ((), ())), preferred_element_t...  1.47 us
    ge x1, other arithmetic, per_device(): frame_slots >= 0  0.8 us
  transfers between devices with their start and end apart: 2, of which 2 were waited for; matrix products, arithmetic and copies ran while one was open for 6% of the time, Pallas kernels for 0%

profile of v1, /device:TPU:0, one launch (start us, length us, event | category | flops | bytes accessed | tf_op | source)
XLA Modules:
  0.0 38.5 jit_solution(886269594946987317)
XLA Ops:
  0.6 0.0 copy-start
  0.6 0.8 %broadcast_compare_fusion = pred[2,16]{1,0:T(4,128)(4,1)S(1)} fusion(s32[2,16]{1,0:T(2,128)} %param.5), kind=kLoop, calls=%fused_computation.42 | loop fusion | flops 32 | bytes 160 | tf_op jit(solution)/shard_map/ge | solution.py:27
  1.5 0.1 broadcast_in_dim.56
  1.6 0.5 %copy-done = bf16[2,16,49,512]{3,1,2,0:T(8,128)(2,1)S(1)} copy-done((bf16[2,16,49,512]{3,1,2,0:T(8,128)(2,1)S(1)}, bf16[2,16,49,512]{3,1,2,0:T(8,128)(2,1)}, u32[]{:S(2)}) %copy-start) | copy-done | bytes 1605656
  2.1 1.5 %convolution_multiply_fusion.1 = f32[1568,128]{1,0:T(8,128)S(1)} fusion(bf16[1568,512]{1,0:T(8,128)(2,1)S(1)} %bitcast.61, bf16[128,512]{1,0:T(8,128)(2,1)} %param.3), kind=kOutput, calls=%fused_computation.2 | convolution fusion | flops 205721600 | bytes 2539520 | tf_op jit(solution)/shard_map/dot_general | solution.py:30
  3.6 0.3 select_reduce_fusion
  3.8 0.3 fusion.6
  4.2 0.7 %broadcast_in_dim.60 = f32[32,6,128]{2,1,0:T(8,128)} broadcast(f32[6,128]{1,0:T(8,128)S(1)} %pad_maximum_fusion), dimensions={1,2} | broadcast | bytes 101376 | tf_op jit(solution)/shard_map/broadcast_in_dim | solution.py:40
  4.8 7.3 %all-to-all-start = ((f32[32,6,128]{2,1,0:T(8,128)}), f32[32,6,128]{2,1,0:T(8,128)S(1)}, u32[]{:S(2)}, u32[]{:S(2)}) async-start(f32[32,6,128]{2,1,0:T(8,128)} %broadcast_in_dim.60), calls=%async_computation | async-start | bytes 262144 | tf_op jit(solution)/shard_map/all_to_all | solution.py:41
  12.2 0.1 broadcast_in_dim.62
  12.3 8.1 %all-to-all-done = f32[32,6,128]{2,1,0:T(8,128)S(1)} async-done(((f32[32,6,128]{2,1,0:T(8,128)}), f32[32,6,128]{2,1,0:T(8,128)S(1)}, u32[]{:S(2)}, u32[]{:S(2)}) %all-to-all-start) | async-done | bytes 98336 | tf_op jit(solution)/shard_map/all_to_all | solution.py:41
  20.4 0.1 fusion.8
  20.5 0.1 div.40
  20.7 0.1 reduce_sum.105
  20.8 0.6 %select_reduce_fusion.1 = (f32[]{:T(128)}, f32[16]{0:T(128)S(1)}, f32[16]{0:T(128)S(1)}) fusion(f32[16,16]{1,0:T(8,128)S(1)} %reduce_sum.105, f32[16]{0:T(128)S(1)} %multiply_reduce_fusion.2), kind=kLoop, calls=%fused_computation.27 | loop fusion | flops 1759 | bytes 1220 | tf_op jit(solution)/shard_map/reduce_sum | solution.py:64
  21.4 0.2 fusion.13
  21.6 0.1 subtract_multiply_fusion
  21.7 0.1 copy.18
  21.8 0.1 constant_dynamic-slice_fusion.2
  21.8 0.1 copy.19
  21.9 0.3 fusion.2
  22.3 0.0 copy-start.1
  22.3 0.4 %convolution_multiply_fusion.2 = f32[128,512]{1,0:T(8,128)S(1)} fusion(bf16[1568,128]{1,0:T(8,128)(2,1)S(1)} %fusion.2, bf16[1568,512]{1,0:T(8,128)(2,1)S(1)} %bitcast.62), kind=kOutput, calls=%fused_computation.3 | convolution fusion | flops 205586432 | bytes 2269184 | tf_op jit(solution)/shard_map/dot_general | solution.py:77
  22.7 0.8 %reshape.72 = f32[32,4,512]{2,1,0:T(4,128)} reshape(f32[128,512]{1,0:T(8,128)S(1)} %convolution_multiply_fusion.2) | data formatting | bytes 524288 | tf_op jit(solution)/shard_map/reshape | solution.py:80
  23.5 2.6 %all-to-all-start.1 = ((f32[32,4,512]{2,1,0:T(4,128)}), f32[32,4,512]{2,1,0:T(4,128)S(1)}, u32[]{:S(2)}, u32[]{:S(2)}) async-start(f32[32,4,512]{2,1,0:T(4,128)} %reshape.72), calls=%async_computation.1 | async-start | bytes 524288 | tf_op jit(solution)/shard_map/all_to_all | solution.py:81
  26.7 0.6 %add_reduce_fusion = (f32[]{:T(128)}, f32[]{:T(128)}) fusion(f32[16]{0:T(128)S(1)} %get-tuple-element.9, f32[16]{0:T(128)S(1)} %fusion.13, f32[16]{0:T(128)S(1)} %multiply_reduce_fusion.2, f32[16]{0:T(128)S(1)} %get-tuple-element.8), kind=kLoop, calls=%fused_computation.40 | loop fusion | flops 62 | bytes 264 | tf_op jit(solution)/shard_map/reduce_sum | solution.py:66
  28.7 0.0 copy-done.1
  28.7 1.7 %fusion = bf16[1568,512]{1,0:T(8,128)(2,1)} fusion(bf16[1568,128]{1,0:T(8,128)(2,1)S(1)} %fusion.2, bf16[128,512]{1,0:T(8,128)(2,1)S(1)} %copy-done.1), kind=kOutput, calls=%fused_computation.1 | convolution fusion | flops 207126528 | bytes 2138112 | tf_op jit(solution)/shard_map/dot_general | solution.py:83
  30.4 6.3 %all-to-all-done.1 = f32[32,4,512]{2,1,0:T(4,128)S(1)} async-done(((f32[32,4,512]{2,1,0:T(4,128)}), f32[32,4,512]{2,1,0:T(4,128)S(1)}, u32[]{:S(2)}, u32[]{:S(2)}) %all-to-all-start.1) | async-done | bytes 262176 | tf_op jit(solution)/shard_map/all_to_all | solution.py:81
  36.7 0.7 %reduce_sum.112 = f32[4,512]{1,0:T(4,128)} reduce(f32[32,4,512]{2,1,0:T(4,128)S(1)} %all-to-all-done.1, f32[]{:T(128)} %constant.18.clone.1), dimensions={0}, to_apply=%region_14.15 | reduce | flops 63488 | bytes 270340 | tf_op jit(solution)/shard_map/reduce_sum | solution.py:82
  (12 shorter events, 0.1 us)
Async XLA Ops:
  0.6 1.4 %copy-start = (bf16[2,16,49,512]{3,1,2,0:T(8,128)(2,1)S(1)}, bf16[2,16,49,512]{3,1,2,0:T(8,128)(2,1)}, u32[]{:S(2)}) copy-start(bf16[2,16,49,512]{3,1,2,0:T(8,128)(2,1)} %param.4) | copy-start | bytes 4816900
  4.8 15.5 %all-to-all-start = ((f32[32,6,128]{2,1,0:T(8,128)}), f32[32,6,128]{2,1,0:T(8,128)S(1)}, u32[]{:S(2)}, u32[]{:S(2)}) async-start(f32[32,6,128]{2,1,0:T(8,128)} %broadcast_in_dim.60), calls=%async_computation | async-start | bytes 262144 | tf_op jit(solution)/shard_map/all_to_all | solution.py:41
  22.3 6.4 %copy-start.1 = (bf16[128,512]{1,0:T(8,128)(2,1)S(1)}, bf16[128,512]{1,0:T(8,128)(2,1)}, u32[]{:S(2)}) copy-start(bf16[128,512]{1,0:T(8,128)(2,1)} %param.3) | copy-start | bytes 393220
  23.5 13.2 %all-to-all-start.1 = ((f32[32,4,512]{2,1,0:T(4,128)}), f32[32,4,512]{2,1,0:T(4,128)S(1)}, u32[]{:S(2)}, u32[]{:S(2)}) async-start(f32[32,4,512]{2,1,0:T(4,128)} %reshape.72), calls=%async_computation.1 | async-start | bytes 524288 | tf_op jit(solution)/shard_map/all_to_all | solution.py:81

commit v2 on v1

v2 whole, which is shorter than its diff:
```python
import functools

import jax
import jax.numpy as jnp
from jax import lax
from jax.experimental import pallas as pl
from jax.experimental.pallas import tpu as pltpu
from jax.sharding import PartitionSpec as P

WORDS = 8
AXES = ("clip", "cap")

logit_scale = 32.0
loss_scale = 8192.0
big_value = 1e30

F32 = jnp.float32
BF16 = jnp.bfloat16
ANY = pl.BlockSpec(memory_space=pl.ANY)
VMEM = pl.BlockSpec(memory_space=pltpu.VMEM)


FORWARD_PARTS = 1
BACKWARD_PARTS = 2


def row_parts(columns, frame_max, parts):
    patch_rows = columns // frame_max
    edges = [patch_rows * k // parts * frame_max for k in range(parts + 1)]
    return [(a, b - a) for a, b in zip(edges, edges[1:])]


def valid_mask(slots_ref, v, frame_max, lanes):
    count = jnp.int32(0)
    for f in range(frame_max):
        count += (slots_ref[v, f] >= 0).astype(jnp.int32)
    return lax.broadcasted_iota(jnp.int32, (1, frame_max, lanes), 1) < count


def forward_kernel(
    clips, frame_max, scale,
    text_hbm, flat_hbm, slots_hbm,
    stats_ref, scores_ref, flat_ref, text_ref,
    slots_ref, sems,
):
    columns = flat_ref.shape[0] // clips
    lanes = text_ref.shape[0]
    parts = row_parts(columns, frame_max, FORWARD_PARTS)
    runs = [pl.ds(v * columns + start, size) for v in range(clips) for start, size in parts]
    copies = [
        pltpu.make_async_copy(flat_hbm.at[run], flat_ref.at[run], sems.at[k])
        for k, run in enumerate(runs)
    ]
    text_copy = pltpu.make_async_copy(text_hbm, text_ref, sems.at[len(runs)])
    slots_copy = pltpu.make_async_copy(slots_hbm, slots_ref, sems.at[len(runs) + 1])
    text_copy.start()
    slots_copy.start()
    for copy in copies:
        copy.start()
    slots_copy.wait()
    masks = [valid_mask(slots_ref, v, frame_max, lanes) for v in range(clips)]
    text_copy.wait()
    for v in range(clips):
        peak = jnp.full((frame_max, lanes), -big_value, F32)
        for k in range(v * len(parts), (v + 1) * len(parts)):
            copies[k].wait()
            part = lax.dot_general(
                flat_ref[runs[k]], text_ref[...], (((1,), (1,)), ((), ())),
                preferred_element_type=F32,
            ) * scale
            part = jnp.where(masks[v], part.reshape(-1, frame_max, lanes), -big_value)
            scores_ref[runs[k]] = part.reshape(-1, lanes)
            peak = jnp.maximum(peak, jnp.max(part, axis=0))
        peak = jnp.max(peak, axis=0, keepdims=True)
        part = scores_ref[pl.ds(v * columns, columns)].reshape(-1, frame_max, lanes)
        weight = jnp.exp(part - peak[None])
        total = jnp.sum(weight, axis=0)
        weighted = jnp.sum(weight * part, axis=0)
        stats_ref[pl.ds(v, 1)] = peak
        stats_ref[pl.ds(clips + v, 1)] = jnp.sum(total, axis=0, keepdims=True)
        stats_ref[pl.ds(2 * clips + v, 1)] = jnp.sum(weighted, axis=0, keepdims=True)


def caption_mean(row, lanes):
    row = jnp.broadcast_to(row, (8, lanes))
    lane = lax.broadcasted_iota(jnp.int32, (8, lanes), 1)
    step = 1
    while step < WORDS:
        up = pltpu.roll(row, lanes - step, 1)
        down = pltpu.roll(row, step, 1)
        row = row + jnp.where((lane & step) == 0, up, down)
        step *= 2
    return row * (1.0 / WORDS)


def middle_kernel(clips, frame_max, shards, scale, *refs):
    stats = refs[:shards]
    scores_ref, flat_ref, send_ref, slopes_ref = refs[shards:]
    columns = flat_ref.shape[0] // clips
    lanes = scores_ref.shape[1]
    width = flat_ref.shape[1]
    devices, own_rows, _ = send_ref.shape
    group = WORDS // clips
    lane = lax.broadcasted_iota(jnp.int32, (8, lanes), 1)
    means = None
    for v in range(clips):
        peaks = [s[pl.ds(v, 1)] for s in stats]
        peak = functools.reduce(jnp.maximum, peaks)
        factors = [jnp.exp(p - peak) for p in peaks]
        total = sum(f * s[pl.ds(clips + v, 1)] for f, s in zip(factors, stats))
        pooled = sum(f * s[pl.ds(2 * clips + v, 1)] for f, s in zip(factors, stats)) / total
        inverse = 1.0 / total
        mean = caption_mean(pooled, lanes)
        inside = (lane & (WORDS - 1)) >= v * group
        means = mean if means is None else jnp.where(inside, mean, means)
        rows = pl.ds(v * columns, columns)
        part = scores_ref[rows].reshape(-1, frame_max, lanes)
        slope = jnp.exp(part - peak[None]) * inverse[None] * (1.0 + part - pooled[None])
        slopes_ref[rows] = slope.reshape(columns, lanes)
        grads = lax.dot_general(
            slopes_ref[rows].astype(BF16), flat_ref[rows], (((0,), (0,)), ((), ())),
            preferred_element_type=F32,
        ) * scale
        send_ref[:, :, pl.ds(v * width, width)] = grads.reshape(devices, own_rows, width).astype(BF16)
    high = means.astype(BF16)
    rest = means - high.astype(F32)
    middle = rest.astype(BF16)
    low = (rest - middle.astype(F32)).astype(BF16)
    row = lax.broadcasted_iota(jnp.int32, (own_rows, lanes), 0)
    pieces = [p.astype(F32)[:1] for p in (high, middle, low)]
    block = jnp.where(row == 0, pieces[0], jnp.where(row == 1, pieces[1], jnp.where(row == 2, pieces[2], 0.0)))
    send_ref[:, :, pl.ds(clips * width, lanes)] = jnp.broadcast_to(
        block.astype(BF16)[None], (devices, own_rows, lanes)
    )


def backward_kernel(
    clips, frame_max, shards, scale,
    got_ref, slopes_ref, text_ref,
    loss_hbm, flat_grad_hbm, text_grad_hbm,
    staged_ref, loss_ref, text_grad_ref, sems,
):
    lanes, width = text_ref.shape
    devices, own_rows, _ = got_ref.shape
    owners = devices // shards
    clip_total = owners * clips
    captions = lanes // WORDS
    group = WORDS // clips
    rank = lax.axis_index("clip")
    device = rank * shards + lax.axis_index("cap")
    lane = lax.broadcasted_iota(jnp.int32, (1, lanes), 1)
    word = lane & (WORDS - 1)
    rows = []
    for i in range(owners):
        pieces = got_ref[i * shards, :, pl.ds(clips * width, lanes)].astype(F32)
        rows.append(pieces[0:1] + pieces[1:2] + pieces[2:3])
    packed = jnp.concatenate(rows, axis=0)
    by_clip = []
    for v in range(clips):
        mean = packed
        step = group
        while step < WORDS:
            up = pltpu.roll(mean, lanes - step, 1)
            down = pltpu.roll(mean, step, 1)
            keep = ((word & step) != 0) == ((v * group & step) != 0)
            mean = jnp.where(keep, mean, jnp.where((word & step) == 0, up, down))
            step *= 2
        by_clip.append(logit_scale * mean)
    owner = lax.broadcasted_iota(jnp.int32, (owners, lanes), 0)
    caption = lax.broadcasted_iota(jnp.int32, (owners, lanes), 1) // WORDS
    row_max = functools.reduce(jnp.maximum, [jnp.max(b, axis=0, keepdims=True) for b in by_clip])
    row_exp = [jnp.exp(b - row_max) for b in by_clip]
    row_sum = sum(jnp.sum(e, axis=0, keepdims=True) for e in row_exp)
    per_word = 1.0 / WORDS
    loss = jnp.sum(row_max + jnp.log(row_sum), axis=1, keepdims=True) * per_word
    factor = logit_scale / WORDS * loss_scale * 0.5 / clip_total
    grads = []
    for v in range(clips):
        col_max = jnp.max(by_clip[v], axis=1, keepdims=True)
        col_exp = jnp.exp(by_clip[v] - col_max)
        col_sum = jnp.sum(col_exp, axis=1, keepdims=True) * per_word
        same = caption == owner * clips + v
        loss += jnp.sum(col_max + jnp.log(col_sum), axis=0, keepdims=True)
        matched = jnp.where(same, by_clip[v], 0.0)
        loss -= 2.0 * per_word * jnp.sum(jnp.sum(matched, axis=1, keepdims=True), axis=0, keepdims=True)
        grads.append(
            factor * (row_exp[v] / row_sum + col_exp / col_sum - jnp.where(same, 2.0, 0.0))
        )
    loss_ref[...] = loss * (0.5 / clip_total)
    copies = [pltpu.make_async_copy(loss_ref, loss_hbm, sems.at[0])]
    copies[0].start()

    columns = slopes_ref.shape[0] // clips
    parts = row_parts(columns, frame_max, BACKWARD_PARTS)
    for v in range(clips):
        mine = jnp.sum(jnp.where(owner == rank, grads[v], 0.0), axis=0, keepdims=True)
        for start, size in parts:
            run = pl.ds(v * columns + start, size)
            grad_scores = (slopes_ref[run] * mine).astype(BF16)
            staged_ref[run] = (
                jnp.dot(grad_scores, text_ref[...], preferred_element_type=F32) * scale
            ).astype(BF16)
            copy = pltpu.make_async_copy(
                staged_ref.at[run], flat_grad_hbm.at[run], sems.at[len(copies)]
            )
            copy.start()
            copies.append(copy)
    chosen = lax.broadcasted_iota(jnp.int32, (owners, lanes), 1) == device * own_rows
    out = jnp.zeros((own_rows, width), F32)
    for v in range(clips):
        column = jnp.sum(jnp.where(chosen, grads[v], 0.0), axis=1, keepdims=True)
        for i in range(owners):
            part = jnp.zeros((own_rows, width), F32)
            for k in range(shards):
                part += got_ref[i * shards + k, :, pl.ds(v * width, width)].astype(F32)
            out += column[i : i + 1, :] * part
    text_grad_ref[...] = out
    copies.append(pltpu.make_async_copy(text_grad_ref, text_grad_hbm, sems.at[len(copies)]))
    copies[-1].start()
    for copy in copies:
        copy.wait()


def exchange(value, axis):
    size = lax.axis_size(axis)
    got = []
    for k in range(1, size):
        if size & (size - 1) == 0:
            pairs = [(i, i ^ k) for i in range(size)]
        else:
            pairs = [(i, (i + k) % size) for i in range(size)]
        got.append(lax.ppermute(value, axis, pairs))
    return got


def far(x):
    return pltpu.with_memory_space_constraint(x, pltpu.HBM)


def per_device(text, patches, frame_slots):
    clip_devices = lax.axis_size("clip")
    shards = lax.axis_size("cap")
    devices = clip_devices * shards
    clips, frame_max, patch_rows, width = patches.shape
    text_rows = text.shape[0]
    own_rows = text_rows // devices
    scale = width ** (-0.5)
    flat_rows = clips * patch_rows * frame_max
    assert WORDS % own_rows == 0 and WORDS % clips == 0
    limit = pltpu.CompilerParams(vmem_limit_bytes=24 << 20)

    flat = patches.transpose(0, 2, 1, 3).reshape(flat_rows, width)
    stats, scores, flat_near, text_near = pl.pallas_call(
        functools.partial(forward_kernel, clips, frame_max, scale),
        out_shape=(
            jax.ShapeDtypeStruct((3 * clips, text_rows), F32),
            pltpu.VMEM((flat_rows, text_rows), F32),
            pltpu.VMEM((flat_rows, width), BF16),
            pltpu.VMEM((text_rows, width), BF16),
        ),
        in_specs=[ANY, ANY, ANY],
        out_specs=(VMEM, VMEM, VMEM, VMEM),
        scratch_shapes=[
            pltpu.SMEM(frame_slots.shape, jnp.int32),
            pltpu.SemaphoreType.DMA((clips * FORWARD_PARTS + 2,)),
        ],
        compiler_params=limit,
        name="forward",
    )(far(text), far(flat), far(frame_slots))
    parts = [stats] + exchange(stats, "cap")
    sent, slopes = pl.pallas_call(
        functools.partial(middle_kernel, clips, frame_max, shards, scale),
        out_shape=(
            jax.ShapeDtypeStruct((devices, own_rows, clips * width + text_rows), BF16),
            pltpu.VMEM((flat_rows, text_rows), F32),
        ),
        in_specs=[VMEM] * (shards + 2),
        out_specs=(VMEM, VMEM),
        compiler_params=limit,
        name="middle",
    )(*parts, scores, flat_near)
    got = lax.all_to_all(sent, AXES, split_axis=0, concat_axis=0, tiled=True)
    loss, flat_grad, text_grad = pl.pallas_call(
        functools.partial(backward_kernel, clips, frame_max, shards, scale),
        out_shape=(
            pltpu.HBM((1, 1), F32),
            pltpu.HBM((flat_rows, width), BF16),
            pltpu.HBM((own_rows, width), F32),
        ),
        in_specs=[VMEM, VMEM, VMEM],
        out_specs=(ANY, ANY, ANY),
        scratch_shapes=[
            pltpu.VMEM((flat_rows, width), BF16),
            pltpu.VMEM((1, 1), F32),
            pltpu.VMEM((own_rows, width), F32),
            pltpu.SemaphoreType.DMA((clips * BACKWARD_PARTS + 2,)),
        ],
        compiler_params=limit,
        name="backward",
    )(got, slopes, text_near)
    patch_grad = flat_grad.reshape(clips, patch_rows, frame_max, width).transpose(0, 2, 1, 3)
    return (loss[0, 0], patch_grad, text_grad)


def solution(mesh):
    return jax.shard_map(
        per_device,
        mesh=mesh,
        in_specs=(P(), P("clip", None, "cap", None), P("clip", None)),
        out_specs=(P(), P("clip", None, "cap", None), P(AXES, None)),
        check_vma=False,
    )
```

time: 38.8 us -> 28 us (0.72)
  blocking collectives: 0 us -> 16.2 us
  waiting for transfers between devices: 14.4 us -> 2.93 us
  starting transfers between devices: 9.91 us -> 3.18 us
  Pallas kernels: 0 us -> 4.87 us
  other arithmetic: 4.1 us -> 0 us
  matrix products: 3.63 us -> 0 us
  between operations: 3.89 us -> 0.65 us
  local copies, waits for them, and re-layouts: 2.53 us -> 0 us
    all_to_all x0 -> x1, blocking collectives: none -> 16.2 us  [per_device(): got = lax.all_to_all(sent, AXES, split_axis=0, concat_axis=0, tiled=True)]
    all_to_all x2 -> x0, waiting for transfers between devices: 14.4 us -> none  [the longest x1 8.1 us: per_device(): got = lax.all_to_all(sent, AXES, split_axis=0, concat_axis=0, tiled=True)]
    all_to_all x2 -> x0, starting transfers between devices: 9.91 us -> none  [the longest x1 7.33 us: per_device(): got = lax.all_to_all(sent, AXES, split_axis=0, concat_axis=0, tiled=True)]
    pallas_call x0 -> x3, Pallas kernels: none -> 4.87 us  [the longest x1 2.61 us: per_device(): pl.pallas_call(functools.partial(forward_kernel, clips, frame_max, scale)...]
    dot_general x3 -> x0, matrix products: 3.63 us -> none  [the longest x1 1.72 us: per_device(): lax.dot_general(grad_flat, text, (((1,), (0,)), ((), ())), preferred_elem...]
    ppermute x0 -> x3, starting transfers between devices: none -> 3.18 us  [exchange(): got.append(lax.ppermute(value, axis, pairs))]
    ppermute x0 -> x3, waiting for transfers between devices: none -> 2.93 us  [exchange(): got.append(lax.ppermute(value, axis, pairs))]
    reduce_sum x7 -> x0, other arithmetic: 2.52 us -> none  [the longest x1 0.66 us: per_device(): text_grad = jnp.sum(text_got, axis=0)]
  transfers between devices with their start and end apart: 2 -> 3, of which waited for: 2 -> 2; matrix products, arithmetic and copies ran while one was open for 6% -> 0% of each run, Pallas kernels for 0% -> 0%
where the time goes in v2:
time: 28 us; the launch traced here: 27.8 us
  blocking collectives  16.2 us (58%)
  Pallas kernels  4.87 us (17%)
  starting transfers between devices  3.18 us (11%)
  waiting for transfers between devices  2.93 us (10%)
  between operations  0.65 us (2%)
    all_to_all x1, blocking collectives, per_device(): got = lax.all_to_all(sent, AXES, split_axis=0, concat_axis=0, tiled=True)  16.2 us
    ppermute x3, starting transfers between devices, exchange(): got.append(lax.ppermute(value, axis, pairs))  3.18 us
    ppermute x3, waiting for transfers between devices, exchange(): got.append(lax.ppermute(value, axis, pairs))  2.93 us
    pallas_call x1, Pallas kernels, per_device(): pl.pallas_call(functools.partial(forward_kernel, clips, frame_max, scale)...  2.61 us
    pallas_call x1, Pallas kernels, per_device(): pl.pallas_call(functools.partial(backward_kernel, clips, frame_max, shard...  1.7 us
  transfers between devices with their start and end apart: 3, of which 2 were waited for; matrix products, arithmetic and copies ran while one was open for 0% of the time, Pallas kernels for 0%

profile of v2, /device:TPU:0, one launch (start us, length us, event | category | flops | bytes accessed | tf_op | source)
XLA Modules:
  0.0 27.8 jit_solution(15727760503806475797)
XLA Ops:
  0.6 2.6 %forward.1 = (f32[6,128]{1,0:T(8,128)S(1)}, f32[1568,128]{1,0:T(8,128)S(1)}, bf16[1568,512]{1,0:T(8,128)(2,1)S(1)}, bf16[128,512]{1,0:T(8,128)(2,1)S(1)}) custom-call(bf16[128,512]{1,0:T(8,128)(2,1)} %text_hbm.1, bf16[1568,512]{1,0:T(8,128)(2,1)} %bitcast.7, s32[2,16]{1,0:T(2,128)} %slots_hbm.1), custom_call_target="tpu_custom_call" | custom-call | tf_op jit(solution)/shard_map/forward/pallas_call | solution.py:253
  3.3 2.5 %collective-permute-start.2 = (f32[6,128]{1,0:T(8,128)S(1)}, f32[6,128]{1,0:T(8,128)S(1)}, u32[]{:S(2)}, u32[]{:S(2)}) collective-permute-start(f32[6,128]{1,0:T(8,128)S(1)} %get-tuple-element.12.refs_0_), channel_id=1, source_target_pairs={{0,3},{1,2},{2,1},{3,0},{4,7},{5,6},{6,5},{7,4},{8,11},{9,10},{10,... | collective-permute-start | bytes 9224 | tf_op jit(solution)/shard_map/ppermute | solution.py:232
  5.8 0.6 %collective-permute-start.1 = (f32[6,128]{1,0:T(8,128)S(1)}, f32[6,128]{1,0:T(8,128)S(1)}, u32[]{:S(2)}, u32[]{:S(2)}) collective-permute-start(f32[6,128]{1,0:T(8,128)S(1)} %get-tuple-element.12.refs_0_), channel_id=1, source_target_pairs={{0,2},{1,3},{2,0},{3,1},{4,6},{5,7},{6,4},{7,5},{8,10},{9,11},{10,... | collective-permute-start | bytes 9224 | tf_op jit(solution)/shard_map/ppermute | solution.py:232
  6.4 0.0 collective-permute-start
  6.4 0.7 %collective-permute-done.2.refs_3_ = f32[6,128]{1,0:T(8,128)S(1)} collective-permute-done((f32[6,128]{1,0:T(8,128)S(1)}, f32[6,128]{1,0:T(8,128)S(1)}, u32[]{:S(2)}, u32[]{:S(2)}) %collective-permute-start.2) | collective-permute-done | bytes 3104 | tf_op jit(solution)/shard_map/ppermute | solution.py:232
  7.1 2.3 %collective-permute-done.1.refs_2_ = f32[6,128]{1,0:T(8,128)S(1)} collective-permute-done((f32[6,128]{1,0:T(8,128)S(1)}, f32[6,128]{1,0:T(8,128)S(1)}, u32[]{:S(2)}, u32[]{:S(2)}) %collective-permute-start.1) | collective-permute-done | bytes 3104 | tf_op jit(solution)/shard_map/ppermute | solution.py:232
  9.4 0.0 collective-permute-done.refs_1_
  9.4 0.6 %middle.1 = (bf16[32,4,1152]{2,1,0:T(4,128)(2,1)S(1)}, f32[1568,128]{1,0:T(8,128)S(1)}) custom-call(f32[6,128]{1,0:T(8,128)S(1)} %get-tuple-element.12.refs_0_, f32[6,128]{1,0:T(8,128)S(1)} %collective-permute-done.refs_1_, f32[6,128]{1,0:T(8,128)S(1)} %collective-permute-done.1.refs_2_, f32[6,128]{1,0:T(8,128)S(1)} %collective-permute-done.2.refs_3_, ...), custom_call_target="tpu_custom_call" | custom-call | tf_op jit(solution)/shard_map/middle/pallas_call | solution.py:271
  9.9 16.2 %all_to_all.5.got_ref = bf16[32,4,1152]{2,1,0:T(4,128)(2,1)S(1)} all-to-all(bf16[32,4,1152]{2,1,0:T(4,128)(2,1)S(1)} %get-tuple-element.15), channel_id=1, replica_groups=mesh['clip'=8,'cap'=4] {'clip','cap'}, dimensions={0} | all-to-all | bytes 589824 | tf_op jit(solution)/shard_map/all_to_all | solution.py:282
  26.1 1.7 %backward.1 = (f32[1,1]{1,0:T(1,128)}, bf16[1568,512]{1,0:T(8,128)(2,1)}, f32[4,512]{1,0:T(4,128)}) custom-call(bf16[32,4,1152]{2,1,0:T(4,128)(2,1)S(1)} %all_to_all.5.got_ref, f32[1568,128]{1,0:T(8,128)S(1)} %get-tuple-element.16.slopes_ref, bf16[128,512]{1,0:T(8,128)(2,1)S(1)} %get-tuple-element.17.text_ref), custom_call_target="tpu_custom_call" | custom-call | tf_op jit(solution)/shard_map/backward/pallas_call | solution.py:283
Async XLA Ops:
  3.3 3.8 %collective-permute-start.2 = (f32[6,128]{1,0:T(8,128)S(1)}, f32[6,128]{1,0:T(8,128)S(1)}, u32[]{:S(2)}, u32[]{:S(2)}) collective-permute-start(f32[6,128]{1,0:T(8,128)S(1)} %get-tuple-element.12.refs_0_), channel_id=1, source_target_pairs={{0,3},{1,2},{2,1},{3,0},{4,7},{5,6},{6,5},{7,4},{8,11},{9,10},{10,... | collective-permute-start | bytes 9224 | tf_op jit(solution)/shard_map/ppermute | solution.py:232
  5.8 3.6 %collective-permute-start.1 = (f32[6,128]{1,0:T(8,128)S(1)}, f32[6,128]{1,0:T(8,128)S(1)}, u32[]{:S(2)}, u32[]{:S(2)}) collective-permute-start(f32[6,128]{1,0:T(8,128)S(1)} %get-tuple-element.12.refs_0_), channel_id=1, source_target_pairs={{0,2},{1,3},{2,0},{3,1},{4,6},{5,7},{6,4},{7,5},{8,10},{9,11},{10,... | collective-permute-start | bytes 9224 | tf_op jit(solution)/shard_map/ppermute | solution.py:232
  6.4 3.0 %collective-permute-start = (f32[6,128]{1,0:T(8,128)S(1)}, f32[6,128]{1,0:T(8,128)S(1)}, u32[]{:S(2)}, u32[]{:S(2)}) collective-permute-start(f32[6,128]{1,0:T(8,128)S(1)} %get-tuple-element.12.refs_0_), channel_id=1, source_target_pairs={{0,1},{1,0},{2,3},{3,2},{4,5},{5,4},{6,7},{7,6},{8,9},{9,8},{10,11... | collective-permute-start | bytes 9224 | tf_op jit(solution)/shard_map/ppermute | solution.py:232

commit v3 on v2

v3 whole, which is shorter than its diff:
```python
import functools

import jax
import jax.numpy as jnp
from jax import lax
from jax.experimental import pallas as pl
from jax.experimental.pallas import tpu as pltpu
from jax.sharding import PartitionSpec as P

WORDS = 8
AXES = ("clip", "cap")

logit_scale = 32.0
loss_scale = 8192.0
big_value = 1e30

F32 = jnp.float32
BF16 = jnp.bfloat16
ANY = pl.BlockSpec(memory_space=pl.ANY)
VMEM = pl.BlockSpec(memory_space=pltpu.VMEM)


BACKWARD_PARTS = 2
SCORE_PARTS = 2


def row_parts(columns, frame_max, parts):
    patch_rows = columns // frame_max
    edges = [patch_rows * k // parts * frame_max for k in range(parts + 1)]
    return [(a, b - a) for a, b in zip(edges, edges[1:])]


def valid_mask(slots_ref, v, frame_max, lanes):
    count = jnp.int32(0)
    for f in range(frame_max):
        count += (slots_ref[v, f] >= 0).astype(jnp.int32)
    return lax.broadcasted_iota(jnp.int32, (1, frame_max, lanes), 1) < count


def own_half(rows, own_rows):
    split = rows.reshape(-1, 2, own_rows, rows.shape[-1])
    even_rows = split[:, 0].reshape(-1, rows.shape[-1])
    odd_rows = split[:, 1].reshape(-1, rows.shape[-1])
    odd = (lax.axis_index("cap") & 1) == 1
    return jnp.where(odd, odd_rows, even_rows), jnp.where(odd, even_rows, odd_rows)


def forward_kernel(
    clips, frame_max, own_rows, scale,
    text_hbm, flat_hbm, slots_hbm,
    stats_ref, scores_ref, text_ref, give_ref, keep_ref,
    flat_ref, slots_ref, sems,
):
    columns, width = flat_ref.shape[0] // clips, flat_ref.shape[1]
    lanes = text_ref.shape[0]
    runs = [pl.ds(v * columns, columns) for v in range(clips)]
    copies = [
        pltpu.make_async_copy(flat_hbm.at[run], flat_ref.at[run], sems.at[v])
        for v, run in enumerate(runs)
    ]
    text_copy = pltpu.make_async_copy(text_hbm, text_ref, sems.at[clips])
    slots_copy = pltpu.make_async_copy(slots_hbm, slots_ref, sems.at[clips + 1])
    text_copy.start()
    slots_copy.start()
    for copy in copies:
        copy.start()
    slots_copy.wait()
    masks = [valid_mask(slots_ref, v, frame_max, lanes) for v in range(clips)]
    text_copy.wait()

    def score(v):
        peak = jnp.full((frame_max, lanes), -big_value, F32)
        for start, size in row_parts(columns, frame_max, SCORE_PARTS):
            run = pl.ds(v * columns + start, size)
            part = lax.dot_general(
                flat_ref[run], text_ref[...], (((1,), (1,)), ((), ())), preferred_element_type=F32
            ) * scale
            part = jnp.where(masks[v], part.reshape(-1, frame_max, lanes), -big_value)
            scores_ref[run] = part.reshape(-1, lanes)
            peak = jnp.maximum(peak, jnp.max(part, axis=0))
        return jnp.max(peak, axis=0, keepdims=True)

    def pool(v, peak):
        part = scores_ref[runs[v]].reshape(-1, frame_max, lanes)
        weight = jnp.exp(part - peak[None])
        total = jnp.sum(jnp.sum(weight, axis=0), axis=0, keepdims=True)
        weighted = jnp.sum(jnp.sum(weight * part, axis=0), axis=0, keepdims=True)
        stats_ref[pl.ds(v, 1)] = peak
        stats_ref[pl.ds(clips + v, 1)] = total
        stats_ref[pl.ds(2 * clips + v, 1)] = weighted
        slope = weight * (1.0 + part - (weighted / total)[None])
        both = jnp.concatenate(
            [slope.reshape(columns, lanes).astype(BF16), weight.reshape(columns, lanes).astype(BF16)],
            axis=1,
        )
        grads = lax.dot_general(
            both, flat_ref[runs[v]], (((0,), (0,)), ((), ())), preferred_element_type=F32
        ) * scale
        for q in range(2):
            keep, give = own_half(grads[q * lanes : (q + 1) * lanes], own_rows)
            span = pl.ds((2 * v + q) * width, width)
            keep_ref[:, span] = keep
            give_ref[:, span] = give

    peaks = []
    for v in range(clips):
        copies[v].wait()
        peaks.append(score(v))
    for v in range(clips):
        pool(v, peaks[v])


def caption_mean(row, lanes):
    row = jnp.broadcast_to(row, (8, lanes))
    lane = lax.broadcasted_iota(jnp.int32, (8, lanes), 1)
    step = 1
    while step < WORDS:
        up = pltpu.roll(row, lanes - step, 1)
        down = pltpu.roll(row, step, 1)
        row = row + jnp.where((lane & step) == 0, up, down)
        step *= 2
    return row * (1.0 / WORDS)


def merge(clips, stats, v):
    peaks = [s[pl.ds(v, 1)] for s in stats]
    totals = [s[pl.ds(clips + v, 1)] for s in stats]
    weighted = [s[pl.ds(2 * clips + v, 1)] for s in stats]
    peak = functools.reduce(jnp.maximum, peaks)
    factors = [jnp.exp(p - peak) for p in peaks]
    inverse = 1.0 / sum(f * t for f, t in zip(factors, totals))
    pooled = sum(f * w for f, w in zip(factors, weighted)) * inverse
    shares = [(f * inverse, w / t - pooled) for f, w, t in zip(factors, weighted, totals)]
    return peak, inverse, pooled, shares


def pack_kernel(clips, shards, *refs):
    stats = refs[:shards]
    keep_ref, got_ref, send_ref = refs[shards:]
    pairs, own_rows, _ = send_ref.shape
    width = keep_ref.shape[1] // (2 * clips)
    lanes = stats[0].shape[1]
    group = WORDS // clips
    lane = lax.broadcasted_iota(jnp.int32, (8, lanes), 1)
    means = None
    columns = []
    for v in range(clips):
        _, _, pooled, shares = merge(clips, stats, v)
        mean = caption_mean(pooled, lanes)
        inside = (lane & (WORDS - 1)) >= v * group
        means = mean if means is None else jnp.where(inside, mean, means)
        for factor, shift in shares[:2]:
            columns += [factor, factor * shift]
    fill = -len(columns) % 8
    columns += [jnp.zeros((1, lanes), F32)] * fill
    columns, _ = own_half(jnp.concatenate(columns, axis=0).T, own_rows)
    for v in range(clips):
        out = None
        for n, ref in enumerate((keep_ref, got_ref)):
            for q in range(2):
                k = 4 * v + 2 * n + q
                term = columns[:, k : k + 1] * ref[:, pl.ds((2 * v + q) * width, width)]
                out = term if out is None else out + term
        send_ref[:, :, pl.ds(v * width, width)] = out.reshape(pairs, own_rows, width).astype(BF16)
    high = means.astype(BF16)
    rest = means - high.astype(F32)
    middle = rest.astype(BF16)
    low = (rest - middle.astype(F32)).astype(BF16)
    row = lax.broadcasted_iota(jnp.int32, (own_rows, lanes), 0)
    pieces = [p.astype(F32)[:1] for p in (high, middle, low)]
    block = jnp.where(row == 0, pieces[0], jnp.where(row == 1, pieces[1], jnp.where(row == 2, pieces[2], 0.0)))
    send_ref[:, :, pl.ds(clips * width, lanes)] = jnp.broadcast_to(
        block.astype(BF16)[None], (pairs, own_rows, lanes)
    )


def backward_kernel(
    clips, frame_max, shards, scale,
    got_ref, scores_ref, text_ref, *refs,
):
    stats = refs[:shards]
    loss_hbm, flat_grad_hbm, text_grad_hbm, staged_ref, loss_ref, text_grad_ref, sems = refs[shards:]
    lanes, width = text_ref.shape
    senders, own_rows, _ = got_ref.shape
    owners = lax.axis_size("clip")
    shares = senders // owners
    clip_total = owners * clips
    captions = lanes // WORDS
    group = WORDS // clips
    rank = lax.axis_index("clip")
    device = rank * shards + lax.axis_index("cap")
    lane = lax.broadcasted_iota(jnp.int32, (1, lanes), 1)
    word = lane & (WORDS - 1)
    rows = []
    for i in range(owners):
        pieces = got_ref[i * shares, :, pl.ds(clips * width, lanes)].astype(F32)
        rows.append(pieces[0:1] + pieces[1:2] + pieces[2:3])
    packed = jnp.concatenate(rows, axis=0)
    by_clip = []
    for v in range(clips):
        mean = packed
        step = group
        while step < WORDS:
            up = pltpu.roll(mean, lanes - step, 1)
            down = pltpu.roll(mean, step, 1)
            keep = ((word & step) != 0) == ((v * group & step) != 0)
            mean = jnp.where(keep, mean, jnp.where((word & step) == 0, up, down))
            step *= 2
        by_clip.append(logit_scale * mean)
    owner = lax.broadcasted_iota(jnp.int32, (owners, lanes), 0)
    caption = lax.broadcasted_iota(jnp.int32, (owners, lanes), 1) // WORDS
    row_max = functools.reduce(jnp.maximum, [jnp.max(b, axis=0, keepdims=True) for b in by_clip])
    row_exp = [jnp.exp(b - row_max) for b in by_clip]
    row_sum = sum(jnp.sum(e, axis=0, keepdims=True) for e in row_exp)
    per_word = 1.0 / WORDS
    loss = jnp.sum(row_max + jnp.log(row_sum), axis=1, keepdims=True) * per_word
    factor = logit_scale / WORDS * loss_scale * 0.5 / clip_total
    grads = []
    for v in range(clips):
        col_max = jnp.max(by_clip[v], axis=1, keepdims=True)
        col_exp = jnp.exp(by_clip[v] - col_max)
        col_sum = jnp.sum(col_exp, axis=1, keepdims=True) * per_word
        same = caption == owner * clips + v
        loss += jnp.sum(col_max + jnp.log(col_sum), axis=0, keepdims=True)
        matched = jnp.where(same, by_clip[v], 0.0)
        loss -= 2.0 * per_word * jnp.sum(jnp.sum(matched, axis=1, keepdims=True), axis=0, keepdims=True)
        grads.append(
            factor * (row_exp[v] / row_sum + col_exp / col_sum - jnp.where(same, 2.0, 0.0))
        )
    loss_ref[...] = loss * (0.5 / clip_total)
    copies = [pltpu.make_async_copy(loss_ref, loss_hbm, sems.at[0])]
    copies[0].start()

    columns = scores_ref.shape[0] // clips
    parts = row_parts(columns, frame_max, BACKWARD_PARTS)
    for v in range(clips):
        mine = jnp.sum(jnp.where(owner == rank, grads[v], 0.0), axis=0, keepdims=True)
        peak, inverse, pooled, _ = merge(clips, stats, v)
        mine = mine * inverse
        for start, size in parts:
            run = pl.ds(v * columns + start, size)
            part = scores_ref[run]
            grad_scores = (mine * jnp.exp(part - peak) * (1.0 + part - pooled)).astype(BF16)
            staged_ref[run] = (
                jnp.dot(grad_scores, text_ref[...], preferred_element_type=F32) * scale
            ).astype(BF16)
            copy = pltpu.make_async_copy(
                staged_ref.at[run], flat_grad_hbm.at[run], sems.at[len(copies)]
            )
            copy.start()
            copies.append(copy)
    chosen = lax.broadcasted_iota(jnp.int32, (owners, lanes), 1) == device * own_rows
    out = jnp.zeros((own_rows, width), F32)
    for v in range(clips):
        column = jnp.sum(jnp.where(chosen, grads[v], 0.0), axis=1, keepdims=True)
        for i in range(owners):
            part = jnp.zeros((own_rows, width), F32)
            for k in range(shares):
                part += got_ref[i * shares + k, :, pl.ds(v * width, width)].astype(F32)
            out += column[i : i + 1, :] * part
    text_grad_ref[...] = out
    copies.append(pltpu.make_async_copy(text_grad_ref, text_grad_hbm, sems.at[len(copies)]))
    copies[-1].start()
    for copy in copies:
        copy.wait()


def exchange(value, axis):
    size = lax.axis_size(axis)
    got = []
    for k in range(1, size):
        if size & (size - 1) == 0:
            pairs = [(i, i ^ k) for i in range(size)]
        else:
            pairs = [(i, (i + k) % size) for i in range(size)]
        got.append(lax.ppermute(value, axis, pairs))
    return got


def far(x):
    return pltpu.with_memory_space_constraint(x, pltpu.HBM)


def per_device(text, patches, frame_slots):
    clip_devices = lax.axis_size("clip")
    shards = lax.axis_size("cap")
    devices = clip_devices * shards
    clips, frame_max, patch_rows, width = patches.shape
    text_rows = text.shape[0]
    own_rows = text_rows // devices
    scale = width ** (-0.5)
    flat_rows = clips * patch_rows * frame_max
    pairs = devices // 2
    assert WORDS % own_rows == 0 and WORDS % clips == 0 and shards & (shards - 1) == 0
    assert shards > 1
    limit = pltpu.CompilerParams(vmem_limit_bytes=24 << 20)

    flat = patches.transpose(0, 2, 1, 3).reshape(flat_rows, width)
    stats, scores, text_near, give, keep = pl.pallas_call(
        functools.partial(forward_kernel, clips, frame_max, own_rows, scale),
        out_shape=(
            pltpu.VMEM((3 * clips, text_rows), F32),
            pltpu.VMEM((flat_rows, text_rows), F32),
            pltpu.VMEM((text_rows, width), BF16),
            pltpu.VMEM((text_rows // 2, 2 * clips * width), F32),
            pltpu.VMEM((text_rows // 2, 2 * clips * width), F32),
        ),
        in_specs=[ANY] * 3,
        out_specs=(VMEM,) * 5,
        scratch_shapes=[
            pltpu.VMEM((flat_rows, width), BF16),
            pltpu.SMEM(frame_slots.shape, jnp.int32),
            pltpu.SemaphoreType.DMA((clips + 2,)),
        ],
        compiler_params=limit,
        name="forward",
    )(far(text), far(flat), far(frame_slots))
    got = lax.ppermute(give, AXES, [(d, d ^ 1) for d in range(devices)])
    shares = [stats] + exchange(stats, "cap")
    sent = pl.pallas_call(
        functools.partial(pack_kernel, clips, shards),
        out_shape=pltpu.VMEM((pairs, own_rows, clips * width + text_rows), BF16),
        in_specs=[VMEM] * (shards + 2),
        out_specs=VMEM,
        compiler_params=limit,
        name="pack",
    )(*shares, keep, got)
    halves = [[2 * k + side for k in range(pairs)] for side in range(2)]
    got = lax.all_to_all(
        sent, AXES, split_axis=0, concat_axis=0, tiled=True, axis_index_groups=halves
    )
    loss, flat_grad, text_grad = pl.pallas_call(
        functools.partial(backward_kernel, clips, frame_max, shards, scale),
        out_shape=(
            pltpu.HBM((1, 1), F32),
            pltpu.HBM((flat_rows, width), BF16),
            pltpu.HBM((own_rows, width), F32),
        ),
        in_specs=[VMEM] * (shards + 3),
        out_specs=(ANY, ANY, ANY),
        scratch_shapes=[
            pltpu.VMEM((flat_rows, width), BF16),
            pltpu.VMEM((1, 1), F32),
            pltpu.VMEM((own_rows, width), F32),
            pltpu.SemaphoreType.DMA((clips * BACKWARD_PARTS + 2,)),
        ],
        compiler_params=limit,
        name="backward",
    )(got, scores, text_near, *shares)
    patch_grad = flat_grad.reshape(clips, patch_rows, frame_max, width).transpose(0, 2, 1, 3)
    return (loss[0, 0], patch_grad, text_grad)


def solution(mesh):
    return jax.shard_map(
        per_device,
        mesh=mesh,
        in_specs=(P(), P("clip", None, "cap", None), P("clip", None)),
        out_specs=(P(), P("clip", None, "cap", None), P(AXES, None)),
        check_vma=False,
    )
```

time: 28 us -> 26 us (0.929)
  blocking collectives: 16.2 us -> 13.6 us
  waiting for transfers between devices: 2.93 us -> 3.49 us
    all_to_all x1, blocking collectives: 16.2 us -> 13.6 us  [per_device(): lax.all_to_all(sent, AXES, split_axis=0, concat_axis=0, tiled=True, axis_...]
    ppermute x3, waiting for transfers between devices: 2.93 us -> 3.49 us  [exchange(): got.append(lax.ppermute(value, axis, pairs))]
    ppermute x0 -> x1, starting transfers between devices: none -> 0.56 us  [per_device(): got = lax.ppermute(give, AXES, [(d, d ^ 1) for d in range(devices)])]
    ppermute x3, starting transfers between devices: 3.18 us -> 2.74 us  [exchange(): got.append(lax.ppermute(value, axis, pairs))]
  transfers between devices with their start and end apart: 3 -> 4, of which waited for: 2 -> 2; matrix products, arithmetic and copies ran while one was open for 0% -> 0% of each run, Pallas kernels for 0% -> 0%
where the time goes in v3:
time: 26 us; the launch traced here: 25.9 us
  blocking collectives  13.6 us (52%)
  Pallas kernels  4.86 us (19%)
  waiting for transfers between devices  3.49 us (13%)
  starting transfers between devices  3.29 us (13%)
  between operations  0.65 us (2%)
    all_to_all x1, blocking collectives, per_device(): lax.all_to_all(sent, AXES, split_axis=0, concat_axis=0, tiled=True, axis_...  13.6 us
    ppermute x3, waiting for transfers between devices, exchange(): got.append(lax.ppermute(value, axis, pairs))  3.49 us
    ppermute x3, starting transfers between devices, exchange(): got.append(lax.ppermute(value, axis, pairs))  2.74 us
    pallas_call x1, Pallas kernels, per_device(): pl.pallas_call(functools.partial(forward_kernel, clips, frame_max, own_ro...  2.73 us
    pallas_call x1, Pallas kernels, per_device(): pl.pallas_call(functools.partial(backward_kernel, clips, frame_max, shard...  1.72 us
    ppermute x1, starting transfers between devices, per_device(): got = lax.ppermute(give, AXES, [(d, d ^ 1) for d in range(devices)])  0.56 us
  transfers between devices with their start and end apart: 4, of which 2 were waited for; matrix products, arithmetic and copies ran while one was open for 0% of the time, Pallas kernels for 0%

profile of v3, /device:TPU:0, one launch (start us, length us, event | category | flops | bytes accessed | tf_op | source)
XLA Modules:
  0.0 25.9 jit_solution(3059098188699978662)
XLA Ops:
  0.6 2.7 %forward.1 = (f32[6,128]{1,0:T(8,128)S(1)}, f32[1568,128]{1,0:T(8,128)S(1)}, bf16[128,512]{1,0:T(8,128)(2,1)S(1)}, f32[64,2048]{1,0:T(8,128)S(1)}, f32[64,2048]{1,0:T(8,128)S(1)}) custom-call(bf16[128,512]{1,0:T(8,128)(2,1)} %text_hbm.1, bf16[1568,512]{1,0:T(8,128)(2,1)} %bitcast.7, s32[2,16]{1,0:T(2,128)} %slots_hbm.1), custom_call_target="tpu_custom_call" | custom-call | tf_op jit(solution)/shard_map/forward/pallas_call | solution.py:299
  3.4 0.6 %collective-permute-start.3 = (f32[64,2048]{1,0:T(8,128)S(1)}, f32[64,2048]{1,0:T(8,128)S(1)}, u32[]{:S(2)}, u32[]{:S(2)}) collective-permute-start(f32[64,2048]{1,0:T(8,128)S(1)} %get-tuple-element.13), channel_id=1, source_target_pairs={{0,1},{1,0},{2,3},{3,2},{4,5},{5,4},{6,7},{7,6},{8,9},{9,8},{10,11... | collective-permute-start | bytes 1572872 | tf_op jit(solution)/shard_map/ppermute | solution.py:318
  3.9 2.6 %collective-permute-start.2 = (f32[6,128]{1,0:T(8,128)S(1)}, f32[6,128]{1,0:T(8,128)S(1)}, u32[]{:S(2)}, u32[]{:S(2)}) collective-permute-start(f32[6,128]{1,0:T(8,128)S(1)} %get-tuple-element.11.refs_0_), channel_id=1, source_target_pairs={{0,3},{1,2},{2,1},{3,0},{4,7},{5,6},{6,5},{7,4},{8,11},{9,10},{10,... | collective-permute-start | bytes 9224 | tf_op jit(solution)/shard_map/ppermute | solution.py:276
  6.5 0.0 collective-permute-start.1
  6.6 0.1 collective-permute-start
  6.7 1.2 %collective-permute-done.2.refs_3_ = f32[6,128]{1,0:T(8,128)S(1)} collective-permute-done((f32[6,128]{1,0:T(8,128)S(1)}, f32[6,128]{1,0:T(8,128)S(1)}, u32[]{:S(2)}, u32[]{:S(2)}) %collective-permute-start.2) | collective-permute-done | bytes 3104 | tf_op jit(solution)/shard_map/ppermute | solution.py:276
  7.9 2.3 %collective-permute-done.1.refs_2_ = f32[6,128]{1,0:T(8,128)S(1)} collective-permute-done((f32[6,128]{1,0:T(8,128)S(1)}, f32[6,128]{1,0:T(8,128)S(1)}, u32[]{:S(2)}, u32[]{:S(2)}) %collective-permute-start.1) | collective-permute-done | bytes 3104 | tf_op jit(solution)/shard_map/ppermute | solution.py:276
  10.2 0.0 collective-permute-done.refs_1_
  10.2 0.0 collective-permute-done.3.refs_5_
  10.2 0.4 %pack.1 = bf16[16,4,1152]{2,1,0:T(4,128)(2,1)S(1)} custom-call(f32[6,128]{1,0:T(8,128)S(1)} %get-tuple-element.11.refs_0_, f32[6,128]{1,0:T(8,128)S(1)} %collective-permute-done.refs_1_, f32[6,128]{1,0:T(8,128)S(1)} %collective-permute-done.1.refs_2_, f32[6,128]{1,0:T(8,128)S(1)} %collective-permute-done.2.refs_3_, ...), custom_call_target="tpu_custom_call" | custom-call | tf_op jit(solution)/shard_map/pack/pallas_call | solution.py:320
  10.6 13.6 %all_to_all.5.got_ref = bf16[16,4,1152]{2,1,0:T(4,128)(2,1)S(1)} all-to-all(bf16[16,4,1152]{2,1,0:T(4,128)(2,1)S(1)} %pack.1), channel_id=1, replica_groups={{0,2,4,6,8,10,12,14,16,18,20,22,24,26,28,30},{1,3,5,7,9,11,13,15,17,19,..., dimensions={0} | all-to-all | bytes 294912 | tf_op jit(solution)/shard_map/all_to_all | solution.py:329
  24.1 1.7 %backward.1 = (f32[1,1]{1,0:T(1,128)}, bf16[1568,512]{1,0:T(8,128)(2,1)}, f32[4,512]{1,0:T(4,128)}) custom-call(bf16[16,4,1152]{2,1,0:T(4,128)(2,1)S(1)} %all_to_all.5.got_ref, f32[1568,128]{1,0:T(8,128)S(1)} %get-tuple-element.14.scores_ref, bf16[128,512]{1,0:T(8,128)(2,1)S(1)} %get-tuple-element.15.text_ref, f32[6,128]{1,0:T(8,128)S(1)} %get-tuple-element.11.refs_0_, ...), custom_call_target="tpu_custom_call" | custom-call | tf_op jit(solution)/shard_map/backward/pallas_call | solution.py:332
Async XLA Ops:
  3.4 6.8 %collective-permute-start.3 = (f32[64,2048]{1,0:T(8,128)S(1)}, f32[64,2048]{1,0:T(8,128)S(1)}, u32[]{:S(2)}, u32[]{:S(2)}) collective-permute-start(f32[64,2048]{1,0:T(8,128)S(1)} %get-tuple-element.13), channel_id=1, source_target_pairs={{0,1},{1,0},{2,3},{3,2},{4,5},{5,4},{6,7},{7,6},{8,9},{9,8},{10,11... | collective-permute-start | bytes 1572872 | tf_op jit(solution)/shard_map/ppermute | solution.py:318
  3.9 3.9 %collective-permute-start.2 = (f32[6,128]{1,0:T(8,128)S(1)}, f32[6,128]{1,0:T(8,128)S(1)}, u32[]{:S(2)}, u32[]{:S(2)}) collective-permute-start(f32[6,128]{1,0:T(8,128)S(1)} %get-tuple-element.11.refs_0_), channel_id=1, source_target_pairs={{0,3},{1,2},{2,1},{3,0},{4,7},{5,6},{6,5},{7,4},{8,11},{9,10},{10,... | collective-permute-start | bytes 9224 | tf_op jit(solution)/shard_map/ppermute | solution.py:276
  6.5 3.6 %collective-permute-start.1 = (f32[6,128]{1,0:T(8,128)S(1)}, f32[6,128]{1,0:T(8,128)S(1)}, u32[]{:S(2)}, u32[]{:S(2)}) collective-permute-start(f32[6,128]{1,0:T(8,128)S(1)} %get-tuple-element.11.refs_0_), channel_id=1, source_target_pairs={{0,2},{1,3},{2,0},{3,1},{4,6},{5,7},{6,4},{7,5},{8,10},{9,11},{10,... | collective-permute-start | bytes 9224 | tf_op jit(solution)/shard_map/ppermute | solution.py:276
  6.6 3.6 %collective-permute-start = (f32[6,128]{1,0:T(8,128)S(1)}, f32[6,128]{1,0:T(8,128)S(1)}, u32[]{:S(2)}, u32[]{:S(2)}) collective-permute-start(f32[6,128]{1,0:T(8,128)S(1)} %get-tuple-element.11.refs_0_), channel_id=1, source_target_pairs={{0,1},{1,0},{2,3},{3,2},{4,5},{5,4},{6,7},{7,6},{8,9},{9,8},{10,11... | collective-permute-start | bytes 9224 | tf_op jit(solution)/shard_map/ppermute | solution.py:276

commit v4 on v3

--- a/solution.py
+++ b/solution.py
@@ -134,6 +134,10 @@
     return peak, inverse, pooled, shares
 
 
+def pair_slots(pairs):
+    return [(pair + 1) % pairs for pair in range(pairs)]
+
+
 def pack_kernel(clips, shards, *refs):
     stats = refs[:shards]
     keep_ref, got_ref, send_ref = refs[shards:]
@@ -161,7 +165,9 @@
                 k = 4 * v + 2 * n + q
                 term = columns[:, k : k + 1] * ref[:, pl.ds((2 * v + q) * width, width)]
                 out = term if out is None else out + term
-        send_ref[:, :, pl.ds(v * width, width)] = out.reshape(pairs, own_rows, width).astype(BF16)
+        out = out.reshape(pairs, own_rows, width).astype(BF16)
+        for pair, slot in enumerate(pair_slots(pairs)):
+            send_ref[slot, :, pl.ds(v * width, width)] = out[pair]
     high = means.astype(BF16)
     rest = means - high.astype(F32)
     middle = rest.astype(BF16)
@@ -184,8 +190,8 @@
     senders, own_rows, _ = got_ref.shape
     owners = lax.axis_size("clip")
     shares = senders // owners
+    slots = pair_slots(senders)
     clip_total = owners * clips
-    captions = lanes // WORDS
     group = WORDS // clips
     rank = lax.axis_index("clip")
     device = rank * shards + lax.axis_index("cap")
@@ -193,7 +199,7 @@
     word = lane & (WORDS - 1)
     rows = []
     for i in range(owners):
-        pieces = got_ref[i * shares, :, pl.ds(clips * width, lanes)].astype(F32)
+        pieces = got_ref[slots[i * shares], :, pl.ds(clips * width, lanes)].astype(F32)
         rows.append(pieces[0:1] + pieces[1:2] + pieces[2:3])
     packed = jnp.concatenate(rows, axis=0)
     by_clip = []
@@ -256,7 +262,7 @@
         for i in range(owners):
             part = jnp.zeros((own_rows, width), F32)
             for k in range(shares):
-                part += got_ref[i * shares + k, :, pl.ds(v * width, width)].astype(F32)
+                part += got_ref[slots[i * shares + k], :, pl.ds(v * width, width)].astype(F32)
             out += column[i : i + 1, :] * part
     text_grad_ref[...] = out
     copies.append(pltpu.make_async_copy(text_grad_ref, text_grad_hbm, sems.at[len(copies)]))
@@ -325,7 +331,8 @@
         compiler_params=limit,
         name="pack",
     )(*shares, keep, got)
-    halves = [[2 * k + side for k in range(pairs)] for side in range(2)]
+    slots = pair_slots(pairs)
+    halves = [[2 * slots.index(k) + side for k in range(pairs)] for side in range(2)]
     got = lax.all_to_all(
         sent, AXES, split_axis=0, concat_axis=0, tiled=True, axis_index_groups=halves
     )

time: 26 us -> 23.1 us (0.89)
  blocking collectives: 13.6 us -> 10.7 us
    all_to_all x1, blocking collectives: 13.6 us -> 10.7 us  [per_device(): lax.all_to_all(sent, AXES, split_axis=0, concat_axis=0, tiled=True, axis_...]
where the time goes in v4:
time: 23.1 us; the launch traced here: 23 us
  blocking collectives  10.7 us (46%)
  Pallas kernels  4.86 us (21%)
  waiting for transfers between devices  3.49 us (15%)
  starting transfers between devices  3.29 us (14%)
  between operations  0.65 us (3%)
    all_to_all x1, blocking collectives, per_device(): lax.all_to_all(sent, AXES, split_axis=0, concat_axis=0, tiled=True, axis_...  10.7 us
    ppermute x3, waiting for transfers between devices, exchange(): got.append(lax.ppermute(value, axis, pairs))  3.49 us
    ppermute x3, starting transfers between devices, exchange(): got.append(lax.ppermute(value, axis, pairs))  2.74 us
    pallas_call x1, Pallas kernels, per_device(): pl.pallas_call(functools.partial(forward_kernel, clips, frame_max, own_ro...  2.73 us
    pallas_call x1, Pallas kernels, per_device(): pl.pallas_call(functools.partial(backward_kernel, clips, frame_max, shard...  1.73 us
    ppermute x1, starting transfers between devices, per_device(): got = lax.ppermute(give, AXES, [(d, d ^ 1) for d in range(devices)])  0.56 us
  transfers between devices with their start and end apart: 4, of which 2 were waited for; matrix products, arithmetic and copies ran while one was open for 0% of the time, Pallas kernels for 0%

profile of v4, /device:TPU:0, one launch (start us, length us, event | category | flops | bytes accessed | tf_op | source)
XLA Modules:
  0.0 23.0 jit_solution(12540081201123473619)
XLA Ops:
  0.6 2.7 %forward.1 = (f32[6,128]{1,0:T(8,128)S(1)}, f32[1568,128]{1,0:T(8,128)S(1)}, bf16[128,512]{1,0:T(8,128)(2,1)S(1)}, f32[64,2048]{1,0:T(8,128)S(1)}, f32[64,2048]{1,0:T(8,128)S(1)}) custom-call(bf16[128,512]{1,0:T(8,128)(2,1)} %text_hbm.1, bf16[1568,512]{1,0:T(8,128)(2,1)} %bitcast.7, s32[2,16]{1,0:T(2,128)} %slots_hbm.1), custom_call_target="tpu_custom_call" | custom-call | tf_op jit(solution)/shard_map/forward/pallas_call | solution.py:305
  3.4 0.6 %collective-permute-start.3 = (f32[64,2048]{1,0:T(8,128)S(1)}, f32[64,2048]{1,0:T(8,128)S(1)}, u32[]{:S(2)}, u32[]{:S(2)}) collective-permute-start(f32[64,2048]{1,0:T(8,128)S(1)} %get-tuple-element.13), channel_id=1, source_target_pairs={{0,1},{1,0},{2,3},{3,2},{4,5},{5,4},{6,7},{7,6},{8,9},{9,8},{10,11... | collective-permute-start | bytes 1572872 | tf_op jit(solution)/shard_map/ppermute | solution.py:324
  3.9 2.6 %collective-permute-start.2 = (f32[6,128]{1,0:T(8,128)S(1)}, f32[6,128]{1,0:T(8,128)S(1)}, u32[]{:S(2)}, u32[]{:S(2)}) collective-permute-start(f32[6,128]{1,0:T(8,128)S(1)} %get-tuple-element.11.refs_0_), channel_id=1, source_target_pairs={{0,3},{1,2},{2,1},{3,0},{4,7},{5,6},{6,5},{7,4},{8,11},{9,10},{10,... | collective-permute-start | bytes 9224 | tf_op jit(solution)/shard_map/ppermute | solution.py:282
  6.5 0.0 collective-permute-start.1
  6.6 0.1 collective-permute-start
  6.7 1.2 %collective-permute-done.2.refs_3_ = f32[6,128]{1,0:T(8,128)S(1)} collective-permute-done((f32[6,128]{1,0:T(8,128)S(1)}, f32[6,128]{1,0:T(8,128)S(1)}, u32[]{:S(2)}, u32[]{:S(2)}) %collective-permute-start.2) | collective-permute-done | bytes 3104 | tf_op jit(solution)/shard_map/ppermute | solution.py:282
  7.9 2.3 %collective-permute-done.1.refs_2_ = f32[6,128]{1,0:T(8,128)S(1)} collective-permute-done((f32[6,128]{1,0:T(8,128)S(1)}, f32[6,128]{1,0:T(8,128)S(1)}, u32[]{:S(2)}, u32[]{:S(2)}) %collective-permute-start.1) | collective-permute-done | bytes 3104 | tf_op jit(solution)/shard_map/ppermute | solution.py:282
  10.2 0.0 collective-permute-done.refs_1_
  10.2 0.0 collective-permute-done.3.refs_5_
  10.2 0.4 %pack.1 = bf16[16,4,1152]{2,1,0:T(4,128)(2,1)S(1)} custom-call(f32[6,128]{1,0:T(8,128)S(1)} %get-tuple-element.11.refs_0_, f32[6,128]{1,0:T(8,128)S(1)} %collective-permute-done.refs_1_, f32[6,128]{1,0:T(8,128)S(1)} %collective-permute-done.1.refs_2_, f32[6,128]{1,0:T(8,128)S(1)} %collective-permute-done.2.refs_3_, ...), custom_call_target="tpu_custom_call" | custom-call | tf_op jit(solution)/shard_map/pack/pallas_call | solution.py:326
  10.6 10.7 %all_to_all.5.got_ref = bf16[16,4,1152]{2,1,0:T(4,128)(2,1)S(1)} all-to-all(bf16[16,4,1152]{2,1,0:T(4,128)(2,1)S(1)} %pack.1), channel_id=1, replica_groups={{30,0,2,4,6,8,10,12,14,16,18,20,22,24,26,28},{31,1,3,5,7,9,11,13,15,17,..., dimensions={0} | all-to-all | bytes 294912 | tf_op jit(solution)/shard_map/all_to_all | solution.py:336
  21.2 1.7 %backward.1 = (f32[1,1]{1,0:T(1,128)}, bf16[1568,512]{1,0:T(8,128)(2,1)}, f32[4,512]{1,0:T(4,128)}) custom-call(bf16[16,4,1152]{2,1,0:T(4,128)(2,1)S(1)} %all_to_all.5.got_ref, f32[1568,128]{1,0:T(8,128)S(1)} %get-tuple-element.14.scores_ref, bf16[128,512]{1,0:T(8,128)(2,1)S(1)} %get-tuple-element.15.text_ref, f32[6,128]{1,0:T(8,128)S(1)} %get-tuple-element.11.refs_0_, ...), custom_call_target="tpu_custom_call" | custom-call | tf_op jit(solution)/shard_map/backward/pallas_call | solution.py:339
Async XLA Ops:
  3.4 6.8 %collective-permute-start.3 = (f32[64,2048]{1,0:T(8,128)S(1)}, f32[64,2048]{1,0:T(8,128)S(1)}, u32[]{:S(2)}, u32[]{:S(2)}) collective-permute-start(f32[64,2048]{1,0:T(8,128)S(1)} %get-tuple-element.13), channel_id=1, source_target_pairs={{0,1},{1,0},{2,3},{3,2},{4,5},{5,4},{6,7},{7,6},{8,9},{9,8},{10,11... | collective-permute-start | bytes 1572872 | tf_op jit(solution)/shard_map/ppermute | solution.py:324
  3.9 3.9 %collective-permute-start.2 = (f32[6,128]{1,0:T(8,128)S(1)}, f32[6,128]{1,0:T(8,128)S(1)}, u32[]{:S(2)}, u32[]{:S(2)}) collective-permute-start(f32[6,128]{1,0:T(8,128)S(1)} %get-tuple-element.11.refs_0_), channel_id=1, source_target_pairs={{0,3},{1,2},{2,1},{3,0},{4,7},{5,6},{6,5},{7,4},{8,11},{9,10},{10,... | collective-permute-start | bytes 9224 | tf_op jit(solution)/shard_map/ppermute | solution.py:282
  6.5 3.6 %collective-permute-start.1 = (f32[6,128]{1,0:T(8,128)S(1)}, f32[6,128]{1,0:T(8,128)S(1)}, u32[]{:S(2)}, u32[]{:S(2)}) collective-permute-start(f32[6,128]{1,0:T(8,128)S(1)} %get-tuple-element.11.refs_0_), channel_id=1, source_target_pairs={{0,2},{1,3},{2,0},{3,1},{4,6},{5,7},{6,4},{7,5},{8,10},{9,11},{10,... | collective-permute-start | bytes 9224 | tf_op jit(solution)/shard_map/ppermute | solution.py:282
  6.6 3.6 %collective-permute-start = (f32[6,128]{1,0:T(8,128)S(1)}, f32[6,128]{1,0:T(8,128)S(1)}, u32[]{:S(2)}, u32[]{:S(2)}) collective-permute-start(f32[6,128]{1,0:T(8,128)S(1)} %get-tuple-element.11.refs_0_), channel_id=1, source_target_pairs={{0,1},{1,0},{2,3},{3,2},{4,5},{5,4},{6,7},{7,6},{8,9},{9,8},{10,11... | collective-permute-start | bytes 9224 | tf_op jit(solution)/shard_map/ppermute | solution.py:282

commit v5 on v4

--- a/solution.py
+++ b/solution.py
@@ -134,11 +134,19 @@
     return peak, inverse, pooled, shares
 
 
-def pair_slots(pairs):
-    return [(pair + 1) % pairs for pair in range(pairs)]
-
-
-def pack_kernel(clips, shards, *refs):
+def pair_order(mesh):
+    places = [getattr(d, "coords", (n // 2,)) for n, d in enumerate(mesh.devices.flat)][::2]
+    spans = [max(axis) + 1 for axis in zip(*places)]
+
+    def apart(one, two):
+        steps = [abs(a - b) for a, b in zip(one, two)]
+        return sum(min(step, span - step) for step, span in zip(steps, spans))
+
+    lead = max(places, key=lambda place: apart(place, places[0]))
+    return sorted(range(len(places)), key=lambda pair: apart(places[pair], lead))
+
+
+def pack_kernel(clips, shards, order, *refs):
     stats = refs[:shards]
     keep_ref, got_ref, send_ref = refs[shards:]
     pairs, own_rows, _ = send_ref.shape
@@ -166,7 +174,7 @@
                 term = columns[:, k : k + 1] * ref[:, pl.ds((2 * v + q) * width, width)]
                 out = term if out is None else out + term
         out = out.reshape(pairs, own_rows, width).astype(BF16)
-        for pair, slot in enumerate(pair_slots(pairs)):
+        for slot, pair in enumerate(order):
             send_ref[slot, :, pl.ds(v * width, width)] = out[pair]
     high = means.astype(BF16)
     rest = means - high.astype(F32)
@@ -181,7 +189,7 @@
 
 
 def backward_kernel(
-    clips, frame_max, shards, scale,
+    clips, frame_max, shards, order, scale,
     got_ref, scores_ref, text_ref, *refs,
 ):
     stats = refs[:shards]
@@ -190,7 +198,7 @@
     senders, own_rows, _ = got_ref.shape
     owners = lax.axis_size("clip")
     shares = senders // owners
-    slots = pair_slots(senders)
+    slots = [order.index(pair) for pair in range(senders)]
     clip_total = owners * clips
     group = WORDS // clips
     rank = lax.axis_index("clip")
@@ -287,7 +295,7 @@
     return pltpu.with_memory_space_constraint(x, pltpu.HBM)
 
 
-def per_device(text, patches, frame_slots):
+def per_device(order, text, patches, frame_slots):
     clip_devices = lax.axis_size("clip")
     shards = lax.axis_size("cap")
     devices = clip_devices * shards
@@ -324,20 +332,19 @@
     got = lax.ppermute(give, AXES, [(d, d ^ 1) for d in range(devices)])
     shares = [stats] + exchange(stats, "cap")
     sent = pl.pallas_call(
-        functools.partial(pack_kernel, clips, shards),
+        functools.partial(pack_kernel, clips, shards, order),
         out_shape=pltpu.VMEM((pairs, own_rows, clips * width + text_rows), BF16),
         in_specs=[VMEM] * (shards + 2),
         out_specs=VMEM,
         compiler_params=limit,
         name="pack",
     )(*shares, keep, got)
-    slots = pair_slots(pairs)
-    halves = [[2 * slots.index(k) + side for k in range(pairs)] for side in range(2)]
+    halves = [[2 * pair + side for pair in order] for side in range(2)]
     got = lax.all_to_all(
         sent, AXES, split_axis=0, concat_axis=0, tiled=True, axis_index_groups=halves
     )
     loss, flat_grad, text_grad = pl.pallas_call(
-        functools.partial(backward_kernel, clips, frame_max, shards, scale),
+        functools.partial(backward_kernel, clips, frame_max, shards, order, scale),
         out_shape=(
             pltpu.HBM((1, 1), F32),
             pltpu.HBM((flat_rows, width), BF16),
@@ -359,8 +366,12 @@
 
 
 def solution(mesh):
+    def step(*args):
+        return per_device(order, *args)
+
+    order = pair_order(mesh)
     return jax.shard_map(
-        per_device,
+        step,
         mesh=mesh,
         in_specs=(P(), P("clip", None, "cap", None), P("clip", None)),
         out_specs=(P(), P("clip", None, "cap", None), P(AXES, None)),

time: 23.1 us -> 23.6 us (1.022)
  blocking collectives: 10.7 us -> 11.2 us
    all_to_all x1, blocking collectives: 10.7 us -> 11.2 us  [per_device(): lax.all_to_all(sent, AXES, split_axis=0, concat_axis=0, tiled=True, axis_...]
where the time goes in v5:
time: 23.6 us; the launch traced here: 23.5 us
  blocking collectives  11.2 us (47%)
  Pallas kernels  4.86 us (21%)
  waiting for transfers between devices  3.49 us (15%)
  starting transfers between devices  3.29 us (14%)
  between operations  0.65 us (3%)
    all_to_all x1, blocking collectives, per_device(): lax.all_to_all(sent, AXES, split_axis=0, concat_axis=0, tiled=True, axis_...  11.2 us
    ppermute x3, waiting for transfers between devices, exchange(): got.append(lax.ppermute(value, axis, pairs))  3.49 us
    ppermute x3, starting transfers between devices, exchange(): got.append(lax.ppermute(value, axis, pairs))  2.74 us
    pallas_call x1, Pallas kernels, per_device(): pl.pallas_call(functools.partial(forward_kernel, clips, frame_max, own_ro...  2.73 us
    pallas_call x1, Pallas kernels, per_device(): pl.pallas_call(functools.partial(backward_kernel, clips, frame_max, shard...  1.72 us
    ppermute x1, starting transfers between devices, per_device(): got = lax.ppermute(give, AXES, [(d, d ^ 1) for d in range(devices)])  0.56 us
  transfers between devices with their start and end apart: 4, of which 2 were waited for; matrix products, arithmetic and copies ran while one was open for 0% of the time, Pallas kernels for 0%

profile of v5, /device:TPU:0, one launch (start us, length us, event | category | flops | bytes accessed | tf_op | source)
XLA Modules:
  0.0 23.5 jit_solution(10328983041550071842)
XLA Ops:
  0.6 2.7 %forward.1 = (f32[6,128]{1,0:T(8,128)S(1)}, f32[1568,128]{1,0:T(8,128)S(1)}, bf16[128,512]{1,0:T(8,128)(2,1)S(1)}, f32[64,2048]{1,0:T(8,128)S(1)}, f32[64,2048]{1,0:T(8,128)S(1)}) custom-call(bf16[128,512]{1,0:T(8,128)(2,1)} %text_hbm.1, bf16[1568,512]{1,0:T(8,128)(2,1)} %bitcast.7, s32[2,16]{1,0:T(2,128)} %slots_hbm.1), custom_call_target="tpu_custom_call" | custom-call | tf_op jit(solution)/shard_map/forward/pallas_call | solution.py:313
  3.4 0.6 %collective-permute-start.3 = (f32[64,2048]{1,0:T(8,128)S(1)}, f32[64,2048]{1,0:T(8,128)S(1)}, u32[]{:S(2)}, u32[]{:S(2)}) collective-permute-start(f32[64,2048]{1,0:T(8,128)S(1)} %get-tuple-element.13), channel_id=1, source_target_pairs={{0,1},{1,0},{2,3},{3,2},{4,5},{5,4},{6,7},{7,6},{8,9},{9,8},{10,11... | collective-permute-start | bytes 1572872 | tf_op jit(solution)/shard_map/ppermute | solution.py:332
  3.9 2.6 %collective-permute-start.2 = (f32[6,128]{1,0:T(8,128)S(1)}, f32[6,128]{1,0:T(8,128)S(1)}, u32[]{:S(2)}, u32[]{:S(2)}) collective-permute-start(f32[6,128]{1,0:T(8,128)S(1)} %get-tuple-element.11.refs_0_), channel_id=1, source_target_pairs={{0,3},{1,2},{2,1},{3,0},{4,7},{5,6},{6,5},{7,4},{8,11},{9,10},{10,... | collective-permute-start | bytes 9224 | tf_op jit(solution)/shard_map/ppermute | solution.py:290
  6.5 0.0 collective-permute-start.1
  6.6 0.1 collective-permute-start
  6.7 1.2 %collective-permute-done.2.refs_3_ = f32[6,128]{1,0:T(8,128)S(1)} collective-permute-done((f32[6,128]{1,0:T(8,128)S(1)}, f32[6,128]{1,0:T(8,128)S(1)}, u32[]{:S(2)}, u32[]{:S(2)}) %collective-permute-start.2) | collective-permute-done | bytes 3104 | tf_op jit(solution)/shard_map/ppermute | solution.py:290
  7.9 2.3 %collective-permute-done.1.refs_2_ = f32[6,128]{1,0:T(8,128)S(1)} collective-permute-done((f32[6,128]{1,0:T(8,128)S(1)}, f32[6,128]{1,0:T(8,128)S(1)}, u32[]{:S(2)}, u32[]{:S(2)}) %collective-permute-start.1) | collective-permute-done | bytes 3104 | tf_op jit(solution)/shard_map/ppermute | solution.py:290
  10.2 0.0 collective-permute-done.refs_1_
  10.2 0.0 collective-permute-done.3.refs_5_
  10.2 0.4 %pack.1 = bf16[16,4,1152]{2,1,0:T(4,128)(2,1)S(1)} custom-call(f32[6,128]{1,0:T(8,128)S(1)} %get-tuple-element.11.refs_0_, f32[6,128]{1,0:T(8,128)S(1)} %collective-permute-done.refs_1_, f32[6,128]{1,0:T(8,128)S(1)} %collective-permute-done.1.refs_2_, f32[6,128]{1,0:T(8,128)S(1)} %collective-permute-done.2.refs_3_, ...), custom_call_target="tpu_custom_call" | custom-call | tf_op jit(solution)/shard_map/pack/pallas_call | solution.py:334
  10.6 11.2 %all_to_all.5.got_ref = bf16[16,4,1152]{2,1,0:T(4,128)(2,1)S(1)} all-to-all(bf16[16,4,1152]{2,1,0:T(4,128)(2,1)S(1)} %pack.1), channel_id=1, replica_groups={{22,14,18,20,30,6,10,12,16,26,28,2,4,8,24,0},{23,15,19,21,31,7,11,13,17..., dimensions={0} | all-to-all | bytes 294912 | tf_op jit(solution)/shard_map/all_to_all | solution.py:343
  21.7 1.7 %backward.1 = (f32[1,1]{1,0:T(1,128)}, bf16[1568,512]{1,0:T(8,128)(2,1)}, f32[4,512]{1,0:T(4,128)}) custom-call(bf16[16,4,1152]{2,1,0:T(4,128)(2,1)S(1)} %all_to_all.5.got_ref, f32[1568,128]{1,0:T(8,128)S(1)} %get-tuple-element.14.scores_ref, bf16[128,512]{1,0:T(8,128)(2,1)S(1)} %get-tuple-element.15.text_ref, f32[6,128]{1,0:T(8,128)S(1)} %get-tuple-element.11.refs_0_, ...), custom_call_target="tpu_custom_call" | custom-call | tf_op jit(solution)/shard_map/backward/pallas_call | solution.py:346
Async XLA Ops:
  3.4 6.8 %collective-permute-start.3 = (f32[64,2048]{1,0:T(8,128)S(1)}, f32[64,2048]{1,0:T(8,128)S(1)}, u32[]{:S(2)}, u32[]{:S(2)}) collective-permute-start(f32[64,2048]{1,0:T(8,128)S(1)} %get-tuple-element.13), channel_id=1, source_target_pairs={{0,1},{1,0},{2,3},{3,2},{4,5},{5,4},{6,7},{7,6},{8,9},{9,8},{10,11... | collective-permute-start | bytes 1572872 | tf_op jit(solution)/shard_map/ppermute | solution.py:332
  3.9 3.9 %collective-permute-start.2 = (f32[6,128]{1,0:T(8,128)S(1)}, f32[6,128]{1,0:T(8,128)S(1)}, u32[]{:S(2)}, u32[]{:S(2)}) collective-permute-start(f32[6,128]{1,0:T(8,128)S(1)} %get-tuple-element.11.refs_0_), channel_id=1, source_target_pairs={{0,3},{1,2},{2,1},{3,0},{4,7},{5,6},{6,5},{7,4},{8,11},{9,10},{10,... | collective-permute-start | bytes 9224 | tf_op jit(solution)/shard_map/ppermute | solution.py:290
  6.5 3.6 %collective-permute-start.1 = (f32[6,128]{1,0:T(8,128)S(1)}, f32[6,128]{1,0:T(8,128)S(1)}, u32[]{:S(2)}, u32[]{:S(2)}) collective-permute-start(f32[6,128]{1,0:T(8,128)S(1)} %get-tuple-element.11.refs_0_), channel_id=1, source_target_pairs={{0,2},{1,3},{2,0},{3,1},{4,6},{5,7},{6,4},{7,5},{8,10},{9,11},{10,... | collective-permute-start | bytes 9224 | tf_op jit(solution)/shard_map/ppermute | solution.py:290
  6.6 3.6 %collective-permute-start = (f32[6,128]{1,0:T(8,128)S(1)}, f32[6,128]{1,0:T(8,128)S(1)}, u32[]{:S(2)}, u32[]{:S(2)}) collective-permute-start(f32[6,128]{1,0:T(8,128)S(1)} %get-tuple-element.11.refs_0_), channel_id=1, source_target_pairs={{0,1},{1,0},{2,3},{3,2},{4,5},{5,4},{6,7},{7,6},{8,9},{9,8},{10,11... | collective-permute-start | bytes 9224 | tf_op jit(solution)/shard_map/ppermute | solution.py:290

commit v6 on v5

--- a/solution.py
+++ b/solution.py
@@ -1,4 +1,5 @@
 import functools
+import math
 
 import jax
 import jax.numpy as jnp
@@ -13,6 +14,8 @@
 logit_scale = 32.0
 loss_scale = 8192.0
 big_value = 1e30
+LOG2E = math.log2(math.e)
+LN2 = math.log(2.0)
 
 F32 = jnp.float32
 BF16 = jnp.bfloat16
@@ -20,7 +23,7 @@
 VMEM = pl.BlockSpec(memory_space=pltpu.VMEM)
 
 
-BACKWARD_PARTS = 2
+BACKWARD_PARTS = 4
 SCORE_PARTS = 2
 
 
@@ -74,7 +77,7 @@
             run = pl.ds(v * columns + start, size)
             part = lax.dot_general(
                 flat_ref[run], text_ref[...], (((1,), (1,)), ((), ())), preferred_element_type=F32
-            ) * scale
+            ) * (scale * LOG2E)
             part = jnp.where(masks[v], part.reshape(-1, frame_max, lanes), -big_value)
             scores_ref[run] = part.reshape(-1, lanes)
             peak = jnp.maximum(peak, jnp.max(part, axis=0))
@@ -82,13 +85,13 @@
 
     def pool(v, peak):
         part = scores_ref[runs[v]].reshape(-1, frame_max, lanes)
-        weight = jnp.exp(part - peak[None])
+        weight = jnp.exp2(part - peak[None])
         total = jnp.sum(jnp.sum(weight, axis=0), axis=0, keepdims=True)
         weighted = jnp.sum(jnp.sum(weight * part, axis=0), axis=0, keepdims=True)
         stats_ref[pl.ds(v, 1)] = peak
         stats_ref[pl.ds(clips + v, 1)] = total
         stats_ref[pl.ds(2 * clips + v, 1)] = weighted
-        slope = weight * (1.0 + part - (weighted / total)[None])
+        slope = weight * (part + (LOG2E - weighted / total)[None])
         both = jnp.concatenate(
             [slope.reshape(columns, lanes).astype(BF16), weight.reshape(columns, lanes).astype(BF16)],
             axis=1,
@@ -127,7 +130,7 @@
     totals = [s[pl.ds(clips + v, 1)] for s in stats]
     weighted = [s[pl.ds(2 * clips + v, 1)] for s in stats]
     peak = functools.reduce(jnp.maximum, peaks)
-    factors = [jnp.exp(p - peak) for p in peaks]
+    factors = [jnp.exp2(p - peak) for p in peaks]
     inverse = 1.0 / sum(f * t for f, t in zip(factors, totals))
     pooled = sum(f * w for f, w in zip(factors, weighted)) * inverse
     shares = [(f * inverse, w / t - pooled) for f, w, t in zip(factors, weighted, totals)]
@@ -158,11 +161,11 @@
     columns = []
     for v in range(clips):
         _, _, pooled, shares = merge(clips, stats, v)
-        mean = caption_mean(pooled, lanes)
+        mean = caption_mean(pooled * LN2, lanes)
         inside = (lane & (WORDS - 1)) >= v * group
         means = mean if means is None else jnp.where(inside, mean, means)
         for factor, shift in shares[:2]:
-            columns += [factor, factor * shift]
+            columns += [factor * LN2, factor * shift * LN2]
     fill = -len(columns) % 8
     columns += [jnp.zeros((1, lanes), F32)] * fill
     columns, _ = own_half(jnp.concatenate(columns, axis=0).T, own_rows)
@@ -250,11 +253,12 @@
     for v in range(clips):
         mine = jnp.sum(jnp.where(owner == rank, grads[v], 0.0), axis=0, keepdims=True)
         peak, inverse, pooled, _ = merge(clips, stats, v)
-        mine = mine * inverse
+        mine = mine * (inverse * LN2)
+        level = LOG2E - pooled
         for start, size in parts:
             run = pl.ds(v * columns + start, size)
             part = scores_ref[run]
-            grad_scores = (mine * jnp.exp(part - peak) * (1.0 + part - pooled)).astype(BF16)
+            grad_scores = (mine * jnp.exp2(part - peak) * (part + level)).astype(BF16)
             staged_ref[run] = (
                 jnp.dot(grad_scores, text_ref[...], preferred_element_type=F32) * scale
             ).astype(BF16)

time: 23.6 us -> 23.6 us (level)
  no operation moved by 1% of the time
where the time goes in v6:
time: 23.6 us; the launch traced here: 23.4 us
  blocking collectives  11.2 us (47%)
  Pallas kernels  4.83 us (20%)
  waiting for transfers between devices  3.49 us (15%)
  starting transfers between devices  3.29 us (14%)
  between operations  0.65 us (3%)
    all_to_all x1, blocking collectives, per_device(): lax.all_to_all(sent, AXES, split_axis=0, concat_axis=0, tiled=True, axis_...  11.2 us
    ppermute x3, waiting for transfers between devices, exchange(): got.append(lax.ppermute(value, axis, pairs))  3.49 us
    ppermute x3, starting transfers between devices, exchange(): got.append(lax.ppermute(value, axis, pairs))  2.73 us
    pallas_call x1, Pallas kernels, per_device(): pl.pallas_call(functools.partial(forward_kernel, clips, frame_max, own_ro...  2.71 us
    pallas_call x1, Pallas kernels, per_device(): pl.pallas_call(functools.partial(backward_kernel, clips, frame_max, shard...  1.71 us
    ppermute x1, starting transfers between devices, per_device(): got = lax.ppermute(give, AXES, [(d, d ^ 1) for d in range(devices)])  0.56 us
  transfers between devices with their start and end apart: 4, of which 2 were waited for; matrix products, arithmetic and copies ran while one was open for 0% of the time, Pallas kernels for 0%

profile of v6, /device:TPU:0, one launch (start us, length us, event | category | flops | bytes accessed | tf_op | source)
XLA Modules:
  0.0 23.4 jit_solution(1347326253894568682)
XLA Ops:
  0.6 2.7 %forward.1 = (f32[6,128]{1,0:T(8,128)S(1)}, f32[1568,128]{1,0:T(8,128)S(1)}, bf16[128,512]{1,0:T(8,128)(2,1)S(1)}, f32[64,2048]{1,0:T(8,128)S(1)}, f32[64,2048]{1,0:T(8,128)S(1)}) custom-call(bf16[128,512]{1,0:T(8,128)(2,1)} %text_hbm.1, bf16[1568,512]{1,0:T(8,128)(2,1)} %bitcast.7, s32[2,16]{1,0:T(2,128)} %slots_hbm.1), custom_call_target="tpu_custom_call" | custom-call | tf_op jit(solution)/shard_map/forward/pallas_call | solution.py:317
  3.3 0.6 %collective-permute-start.3 = (f32[64,2048]{1,0:T(8,128)S(1)}, f32[64,2048]{1,0:T(8,128)S(1)}, u32[]{:S(2)}, u32[]{:S(2)}) collective-permute-start(f32[64,2048]{1,0:T(8,128)S(1)} %get-tuple-element.13), channel_id=1, source_target_pairs={{0,1},{1,0},{2,3},{3,2},{4,5},{5,4},{6,7},{7,6},{8,9},{9,8},{10,11... | collective-permute-start | bytes 1572872 | tf_op jit(solution)/shard_map/ppermute | solution.py:336
  3.9 2.6 %collective-permute-start.2 = (f32[6,128]{1,0:T(8,128)S(1)}, f32[6,128]{1,0:T(8,128)S(1)}, u32[]{:S(2)}, u32[]{:S(2)}) collective-permute-start(f32[6,128]{1,0:T(8,128)S(1)} %get-tuple-element.11.refs_0_), channel_id=1, source_target_pairs={{0,3},{1,2},{2,1},{3,0},{4,7},{5,6},{6,5},{7,4},{8,11},{9,10},{10,... | collective-permute-start | bytes 9224 | tf_op jit(solution)/shard_map/ppermute | solution.py:294
  6.5 0.0 collective-permute-start.1
  6.6 0.1 collective-permute-start
  6.6 1.2 %collective-permute-done.2.refs_3_ = f32[6,128]{1,0:T(8,128)S(1)} collective-permute-done((f32[6,128]{1,0:T(8,128)S(1)}, f32[6,128]{1,0:T(8,128)S(1)}, u32[]{:S(2)}, u32[]{:S(2)}) %collective-permute-start.2) | collective-permute-done | bytes 3104 | tf_op jit(solution)/shard_map/ppermute | solution.py:294
  7.9 2.3 %collective-permute-done.1.refs_2_ = f32[6,128]{1,0:T(8,128)S(1)} collective-permute-done((f32[6,128]{1,0:T(8,128)S(1)}, f32[6,128]{1,0:T(8,128)S(1)}, u32[]{:S(2)}, u32[]{:S(2)}) %collective-permute-start.1) | collective-permute-done | bytes 3104 | tf_op jit(solution)/shard_map/ppermute | solution.py:294
  10.1 0.0 collective-permute-done.refs_1_
  10.1 0.0 collective-permute-done.3.refs_5_
  10.1 0.4 %pack.1 = bf16[16,4,1152]{2,1,0:T(4,128)(2,1)S(1)} custom-call(f32[6,128]{1,0:T(8,128)S(1)} %get-tuple-element.11.refs_0_, f32[6,128]{1,0:T(8,128)S(1)} %collective-permute-done.refs_1_, f32[6,128]{1,0:T(8,128)S(1)} %collective-permute-done.1.refs_2_, f32[6,128]{1,0:T(8,128)S(1)} %collective-permute-done.2.refs_3_, ...), custom_call_target="tpu_custom_call" | custom-call | tf_op jit(solution)/shard_map/pack/pallas_call | solution.py:338
  10.5 11.2 %all_to_all.5.got_ref = bf16[16,4,1152]{2,1,0:T(4,128)(2,1)S(1)} all-to-all(bf16[16,4,1152]{2,1,0:T(4,128)(2,1)S(1)} %pack.1), channel_id=1, replica_groups={{22,14,18,20,30,6,10,12,16,26,28,2,4,8,24,0},{23,15,19,21,31,7,11,13,17..., dimensions={0} | all-to-all | bytes 294912 | tf_op jit(solution)/shard_map/all_to_all | solution.py:347
  21.7 1.7 %backward.1 = (f32[1,1]{1,0:T(1,128)}, bf16[1568,512]{1,0:T(8,128)(2,1)}, f32[4,512]{1,0:T(4,128)}) custom-call(bf16[16,4,1152]{2,1,0:T(4,128)(2,1)S(1)} %all_to_all.5.got_ref, f32[1568,128]{1,0:T(8,128)S(1)} %get-tuple-element.14.scores_ref, bf16[128,512]{1,0:T(8,128)(2,1)S(1)} %get-tuple-element.15.text_ref, f32[6,128]{1,0:T(8,128)S(1)} %get-tuple-element.11.refs_0_, ...), custom_call_target="tpu_custom_call" | custom-call | tf_op jit(solution)/shard_map/backward/pallas_call | solution.py:350
Async XLA Ops:
  3.3 6.8 %collective-permute-start.3 = (f32[64,2048]{1,0:T(8,128)S(1)}, f32[64,2048]{1,0:T(8,128)S(1)}, u32[]{:S(2)}, u32[]{:S(2)}) collective-permute-start(f32[64,2048]{1,0:T(8,128)S(1)} %get-tuple-element.13), channel_id=1, source_target_pairs={{0,1},{1,0},{2,3},{3,2},{4,5},{5,4},{6,7},{7,6},{8,9},{9,8},{10,11... | collective-permute-start | bytes 1572872 | tf_op jit(solution)/shard_map/ppermute | solution.py:336
  3.9 3.9 %collective-permute-start.2 = (f32[6,128]{1,0:T(8,128)S(1)}, f32[6,128]{1,0:T(8,128)S(1)}, u32[]{:S(2)}, u32[]{:S(2)}) collective-permute-start(f32[6,128]{1,0:T(8,128)S(1)} %get-tuple-element.11.refs_0_), channel_id=1, source_target_pairs={{0,3},{1,2},{2,1},{3,0},{4,7},{5,6},{6,5},{7,4},{8,11},{9,10},{10,... | collective-permute-start | bytes 9224 | tf_op jit(solution)/shard_map/ppermute | solution.py:294
  6.5 3.6 %collective-permute-start.1 = (f32[6,128]{1,0:T(8,128)S(1)}, f32[6,128]{1,0:T(8,128)S(1)}, u32[]{:S(2)}, u32[]{:S(2)}) collective-permute-start(f32[6,128]{1,0:T(8,128)S(1)} %get-tuple-element.11.refs_0_), channel_id=1, source_target_pairs={{0,2},{1,3},{2,0},{3,1},{4,6},{5,7},{6,4},{7,5},{8,10},{9,11},{10,... | collective-permute-start | bytes 9224 | tf_op jit(solution)/shard_map/ppermute | solution.py:294
  6.6 3.6 %collective-permute-start = (f32[6,128]{1,0:T(8,128)S(1)}, f32[6,128]{1,0:T(8,128)S(1)}, u32[]{:S(2)}, u32[]{:S(2)}) collective-permute-start(f32[6,128]{1,0:T(8,128)S(1)} %get-tuple-element.11.refs_0_), channel_id=1, source_target_pairs={{0,1},{1,0},{2,3},{3,2},{4,5},{5,4},{6,7},{7,6},{8,9},{9,8},{10,11... | collective-permute-start | bytes 9224 | tf_op jit(solution)/shard_map/ppermute | solution.py:294
